TPU v7x, 256 devices: a whole 4x4x8 slice. The times are simulated.
256 devices in a mesh: dp: 4 (over x_lo, core), space: 64 (over y, z, x_hi).
Axes of the slice: x: 4 (x_hi: 2, x_lo: 2; x = x_hi * 2 + x_lo), y: 4, z: 8, core: 2. Of those that a mesh axis runs over, the one named last changes fastest.
Arguments:
- volume: bfloat16 [4, 512, 32, 2048], P('dp', 'space'), may hold values from -6 to 6
- weight_first: bfloat16 [1728, 128], P('dp'), may hold values from -0.15625 to 0.15625
- weight_second: bfloat16 [3456, 256], P('dp'), may hold values from -0.109375 to 0.109375
- cotangent: bfloat16 [4, 128, 8, 2048], P('dp', 'space'), may hold values from -16 to 16
Outputs:
- activations: bfloat16 [4, 128, 8, 2048], P('dp', 'space')
- input_gradient: bfloat16 [4, 512, 32, 2048], P('dp', 'space')
- first_gradient: float32 [1728, 128], P('dp')
- second_gradient: float32 [3456, 256], P('dp')
All inputs are finite; a program needn't handle non-finite values.
Results may differ from a plain program's by a relative error of at most 0.012.
Values may be sent and summed in bfloat16 or wider, within the bound.
A program may use at most 64 MiB of HBM per device.

v0:
```python
import jax
import jax.numpy as jnp
from jax import lax
from jax.sharding import PartitionSpec as P

CIN = 64
CMID = 128
COUT = 256


LEAK_SLOPE = 0.2
LAYOUT = ("NDHWC", "DHWIO", "NDHWC")


def shifted(x, axis, by):
    length = lax.axis_size(axis)
    pairs = [(i, i + by) for i in range(length) if 0 <= i + by < length]
    return lax.ppermute(x, axis, pairs)


def activate(values):
    return LEAK_SLOPE * values + (1.0 - LEAK_SLOPE) * jax.nn.softplus(values)


def activate_slope(values):
    return LEAK_SLOPE + (1.0 - LEAK_SLOPE) * jax.nn.sigmoid(values)


def pad_sides(tensor):
    return jnp.pad(tensor, ((0, 0), (0, 0), (1, 0), (1, 0), (0, 0)))


def convolve(padded, kernel):
    return lax.conv_general_dilated(
        padded,
        kernel,
        (2, 2, 2),
        ((0, 0), (0, 0), (0, 0)),
        dimension_numbers=LAYOUT,
        preferred_element_type=jnp.float32,
    )


def convolve_back(delta, kernel):
    flipped = jnp.transpose(kernel[::-1, ::-1, ::-1], (0, 1, 2, 4, 3))
    return lax.conv_general_dilated(
        delta,
        flipped,
        (1, 1, 1),
        ((2, 2), (1, 2), (1, 2)),
        lhs_dilation=(2, 2, 2),
        dimension_numbers=LAYOUT,
        preferred_element_type=jnp.float32,
    )


def kernel_gradient(padded, delta):
    channels = padded.shape[-1]
    features = delta.shape[-1]
    tapped = lax.conv_general_dilated(
        padded,
        delta,
        (1, 1, 1),
        ((0, 0), (0, 0), (0, 0)),
        rhs_dilation=(2, 2, 2),
        dimension_numbers=("CDHWN", "IDHWO", "NDHWC"),
        preferred_element_type=jnp.float32,
    )
    return jnp.transpose(tapped, (1, 2, 3, 0, 4)).reshape(27 * channels, features)


def local(volume, weight_first, weight_second, cotangent):
    samples = volume.shape[0]
    planes = volume.shape[1]
    side_cells = volume.shape[2]
    kernel_first = lax.all_gather(weight_first, "dp", axis=0, tiled=True).reshape(
        3, 3, 3, CIN, CMID
    )
    kernel_second = lax.all_gather(weight_second, "dp", axis=0, tiled=True).reshape(
        3, 3, 3, CMID, COUT
    )
    inputs = volume.reshape(samples, planes, side_cells, side_cells, CIN)
    lower_input = shifted(inputs[:, planes - 1 :], "space", 1)
    padded_input = pad_sides(jnp.concatenate([lower_input, inputs], axis=1))
    linear_first = convolve(padded_input, kernel_first)
    hidden = activate(linear_first).astype(jnp.bfloat16)
    half_planes = hidden.shape[1]
    lower_hidden = shifted(hidden[:, half_planes - 1 :], "space", 1)
    padded_hidden = pad_sides(jnp.concatenate([lower_hidden, hidden], axis=1))
    linear_second = convolve(padded_hidden, kernel_second)
    activations = activate(linear_second).astype(jnp.bfloat16)
    incoming = cotangent.reshape(linear_second.shape).astype(jnp.float32)
    delta_second = (incoming * activate_slope(linear_second)).astype(jnp.bfloat16)
    spread = convolve_back(delta_second, kernel_second)
    upper_rim = shifted(spread[:, :1].astype(jnp.bfloat16), "space", -1).astype(jnp.float32)
    hidden_delta = jnp.concatenate([spread[:, 1:-1], spread[:, -1:] + upper_rim], axis=1)
    delta_first = (hidden_delta * activate_slope(linear_first)).astype(jnp.bfloat16)
    spread_input = convolve_back(delta_first, kernel_first)
    upper_input = shifted(spread_input[:, :1].astype(jnp.bfloat16), "space", -1).astype(jnp.float32)
    input_delta = jnp.concatenate(
        [spread_input[:, 1:-1], spread_input[:, -1:] + upper_input], axis=1
    )
    input_gradient = input_delta.astype(jnp.bfloat16)
    tally_first = kernel_gradient(padded_input, delta_first)
    tally_second = kernel_gradient(padded_hidden, delta_second)
    summed = lax.psum((tally_first, tally_second), "space")
    share_first, share_second = (
        lax.psum_scatter(
            summed[0].astype(jnp.bfloat16), "dp", scatter_dimension=0, tiled=True
        ).astype(jnp.float32),
        lax.psum_scatter(
            summed[1].astype(jnp.bfloat16), "dp", scatter_dimension=0, tiled=True
        ).astype(jnp.float32),
    )
    whole_samples = samples * lax.axis_size("dp")
    cells_first = (
        whole_samples
        * linear_first.shape[1]
        * lax.axis_size("space")
        * linear_first.shape[2]
        * linear_first.shape[3]
    )
    cells_second = (
        whole_samples
        * linear_second.shape[1]
        * lax.axis_size("space")
        * linear_second.shape[2]
        * linear_second.shape[3]
    )
    first_gradient = share_first * float(cells_first) ** (-0.5)
    second_gradient = share_second * float(cells_second) ** (-0.5)
    return (
        activations.reshape(cotangent.shape),
        input_gradient.reshape(volume.shape),
        first_gradient,
        second_gradient,
    )


def solution(mesh):
    return jax.shard_map(
        local,
        mesh=mesh,
        in_specs=(
            P("dp", "space", None, None),
            P("dp", None),
            P("dp", None),
            P("dp", "space", None, None),
        ),
        out_specs=(
            P("dp", "space", None, None),
            P("dp", "space", None, None),
            P("dp", None),
            P("dp", None),
        ),
        check_vma=False,
    )
```

profile of v0, /device:TPU:8, one launch (start us, length us, event | category | flops | bytes accessed | tf_op | source)
XLA Modules:
  0.0 578.9 jit_solution(2785918129216724532)
XLA Ops:
  7.2 0.0 all-gather.2.cloned.1.call-start
  7.2 0.7 all-gather.2.cloned.1.call-update
  7.9 0.0 reduce-scatter.3.cloned.1.call-start
  8.0 10.4 %reshape.147 = bf16[1,8,32,32,64]{4,0,3,2,1:T(2,128)(2,1)} reshape(bf16[1,8,32,2048]{3,2,1,0:T(8,128)(2,1)} %param.4) | data formatting | bytes 2097152 | tf_op jit(solution)/shard_map/reshape | solution.py:82
  18.4 1.6 slice.50
  20.0 4.9 collective-permute-start
  24.9 28.4 %all_gather.6 = bf16[1728,128]{1,0:T(8,128)(2,1)S(1)} all-gather(bf16[432,128]{1,0:T(8,128)(2,1)S(1)} %copy-done.4), channel_id=1, replica_groups=mesh['dp'=4,'space'=64] {'dp'}, dimensions={0}, use_global_device_ids=true | all-gather | bytes 552960 | tf_op jit(solution)/shard_map/all_gather | solution.py:76
  53.3 0.5 constant_dynamic-update-slice_fusion.1
  53.8 9.3 %constant_dynamic-update-slice_fusion = bf16[1,9,32,32,64]{4,0,3,2,1:T(2,128)(2,1)S(1)} fusion(bf16[1,9,32,32,64]{4,0,3,2,1:T(2,128)(2,1)S(1)} %constant_dynamic-update-slice_fusion.1, bf16[1,8,32,32,64]{4,0,3,2,1:T(2,128)(2,1)} %reshape.147), kind=kLoop, calls=%fused_computation.59 | loop fusion | bytes 5242880 | tf_op jit(solution)/shard_map/concatenate | solution.py:84
  63.1 2.8 copy.87
  65.9 0.7 pad.4.clone
  66.6 0.0 copy-start.9
  66.6 2.4 copy.41
  69.1 0.8 slice.51
  69.9 2.3 multiply_add_fusion
  72.3 0.1 copy.45
  72.4 0.1 copy.44
  72.5 1.9 collective-permute-start.1
  74.4 0.1 copy.54
  74.6 0.0 copy-start.8
  74.6 0.2 copy.74
  74.8 9.8 %collective-permute-done.1 = bf16[1,1,16,16,128]{4,0,3,2,1:T(2,128)(2,1)S(1)} collective-permute-done((bf16[1,1,16,16,128]{4,0,3,2,1:T(2,128)(2,1)S(1)}, bf16[1,1,16,16,128]{4,0,3,2,1:T(2,128)(2,1)S(1)}, u32[]{:S(2)}, u32[]{:S(2)}) %collective-permute-start.1) | collective-permute-done | bytes 65568 | tf_op jit(solution)/shard_map/ppermute | solution.py:18
  84.6 0.1 constant_dynamic-update-slice_fusion.2
  84.8 0.4 copy_dynamic-update-slice_fusion
  85.3 0.2 pad.6
  85.4 0.1 copy.50
  85.6 0.1 slice.55
  85.7 0.0 all-gather.2.cloned.1.call-done
  85.7 3.1 multiply_add_fusion.1
  88.8 0.2 copy.52
  89.0 4.2 fusion.38
  93.2 0.1 slice.84
  93.3 5.3 collective-permute-start.2
  98.6 3.6 fusion.36
  102.2 0.2 slice_add_fusion
  102.4 0.7 fusion.27
  103.1 11.1 %fusion.50 = f32[3,3,3,64,128]{4,3,2,1,0:T(8,128)S(1)} fusion(bf16[1,9,32,32,64]{4,0,3,2,1:T(2,128)(2,1)S(1)} %bitcast.84, bf16[1,4,16,16,128]{4,0,3,2,1:T(2,128)(2,1)S(1)} %fusion.27), kind=kOutput, calls=%fused_computation.72 | convolution fusion | flops 434307072 | bytes 2326528 | tf_op jit(solution)/shard_map/transpose | solution.py:69
  114.2 387.9 %all-reduce.2 = (bf16[1728,128]{1,0:T(8,128)(2,1)}, bf16[3456,256]{1,0:T(8,128)(2,1)}) all-reduce(f32[1728,128]{1,0:T(8,128)S(1)} %bitcast.97, f32[3456,256]{1,0:T(8,128)} %bitcast.85), channel_id=1, replica_groups=mesh['dp'=4,'space'=64] {'space'}, use_global_device_ids=true, to_apply=%region_0.1 | all-reduce | flops 1105920 | bytes 6635520 | tf_op jit(solution)/shard_map/psum | solution.py:106
  502.1 0.0 reduce-scatter.3.cloned.1.call-update
  502.1 0.0 reduce-scatter.5.cloned.1.call-start
  502.1 0.7 reduce-scatter.5.cloned.1.call-update
  502.8 0.2 copy.89
  503.0 0.1 copy.58
  503.2 3.4 fusion.49
  506.6 0.1 copy.62
  506.7 0.7 slice_bitcast_fusion.1
  507.5 1.9 collective-permute-start.3
  509.4 0.6 slice.56
  510.1 0.5 slice.63
  510.6 0.1 slice.65
  510.6 0.3 copy.61
  510.9 0.7 copy.59
  511.6 0.4 slice.64
  512.0 0.7 copy.60
  512.7 1.5 concatenate.29
  514.2 3.4 collective-permute-done.3
  517.5 1.0 fusion.24
  518.6 0.1 copy.63
  518.7 0.3 concatenate.30
  518.9 1.1 pad_maximum_fusion
  520.0 18.2 %reduce-scatter.3.cloned.1.call-done = bf16[432,128]{1,0:T(8,128)(2,1)} async-done(((bf16[1728,128]{1,0:T(8,128)(2,1)}), bf16[432,128]{1,0:T(8,128)(2,1)}) %reduce-scatter.3.cloned.1.call-update) | async-done | bytes 110608 | tf_op jit(solution)/shard_map/reduce_scatter | solution.py:108
  538.2 1.6 convert_multiply_fusion.1
  539.8 30.4 %reduce-scatter.5.cloned.1.call-done = bf16[864,256]{1,0:T(8,128)(2,1)} async-done(((bf16[3456,256]{1,0:T(8,128)(2,1)}), bf16[864,256]{1,0:T(8,128)(2,1)}) %reduce-scatter.5.cloned.1.call-update) | async-done | bytes 442384 | tf_op jit(solution)/shard_map/reduce_scatter | solution.py:111
  570.2 2.0 convert_multiply_fusion
  (37 shorter events, 0.4 us)
Async XLA Ops:
  7.2 17.7 %copy-start.4 = (bf16[432,128]{1,0:T(8,128)(2,1)S(1)}, bf16[432,128]{1,0:T(8,128)(2,1)}, u32[]{:S(2)}) copy-start(bf16[432,128]{1,0:T(8,128)(2,1)} %param.5) | copy-start | bytes 331780
  7.2 78.5 %all-gather.2.cloned.1.call-start = ((), (), s32[]{:S(2)}) async-start(), calls=%async_computation.2 | async-start | bytes 2211840 | tf_op jit(solution)/shard_map/all_gather | solution.py:79
  7.9 530.3 %reduce-scatter.3.cloned.1.call-start = ((), (), s32[]{:S(2)}) async-start(), calls=%async_computation.3 | async-start | bytes 552960 | tf_op jit(solution)/shard_map/reduce_scatter | solution.py:108
  20.0 33.3 %collective-permute-start = (bf16[1,1,32,32,64]{4,0,3,2,1:T(2,128)(2,1)S(1)}, bf16[1,1,32,32,64]{4,0,3,2,1:T(2,128)(2,1)S(1)}, u32[]{:S(2)}, u32[]{:S(2)}) collective-permute-start(bf16[1,1,32,32,64]{4,0,3,2,1:T(2,128)(2,1)S(1)} %slice.50), channel_id=1, source_target_pairs={{0,1},{1,2},{2,3},{3,4},{4,5},{5,6},{6,7},{7,8},{8,9},{9,10},{10,1... | collective-permute-start | bytes 393224 | tf_op jit(solution)/shard_map/ppermute | solution.py:18
  53.3 16.6 %copy-start.1 = (bf16[1728,128]{1,0:T(8,128)(2,1)}, bf16[1728,128]{1,0:T(8,128)(2,1)S(1)}, u32[]{:S(2)}) copy-start(bf16[1728,128]{1,0:T(8,128)(2,1)S(1)} %all_gather.6) | copy-start | bytes 1327108
  63.1 2.8 copy-start
  66.6 3.3 copy-start.9
  72.5 12.2 %collective-permute-start.1 = (bf16[1,1,16,16,128]{4,0,3,2,1:T(2,128)(2,1)S(1)}, bf16[1,1,16,16,128]{4,0,3,2,1:T(2,128)(2,1)S(1)}, u32[]{:S(2)}, u32[]{:S(2)}) collective-permute-start(bf16[1,1,16,16,128]{4,0,3,2,1:T(2,128)(2,1)S(1)} %copy.44), channel_id=1, source_target_pairs={{0,1},{1,2},{2,3},{3,4},{4,5},{5,6},{6,7},{7,8},{8,9},{9,10},{10,1... | collective-permute-start | bytes 196616 | tf_op jit(solution)/shard_map/ppermute | solution.py:18
  74.6 11.1 %copy-start.8 = (pred[8,2]{0,1:T(4,128)(4,1)S(1)}, pred[8,2]{0,1:T(4,128)(4,1)}, u32[]{:S(2)}) copy-start(pred[8,2]{0,1:T(4,128)(4,1)} %constant.34) | copy-start | bytes 52
  85.7 3.3 copy-start.5
  85.7 3.3 copy-start.7
  93.2 9.9 %slice-start = ((s8[4718592]{0:T(1024)(128)(4,1)}), s8[4194304]{0:T(1024)(128)(4,1)S(1)}, s32[]{:S(2)}) async-start(s8[4718592]{0:T(1024)(128)(4,1)} %bitcast.83), calls=%async_computation.5 | async-start | bytes 8388608
  93.3 9.8 %slice-start.1 = ((s8[4718592]{0:T(1024)(128)(4,1)}), s8[524288]{0:T(1024)(128)(4,1)S(1)}, s32[]{:S(2)}) async-start(s8[4718592]{0:T(1024)(128)(4,1)} %bitcast.83), calls=%async_computation.6 | async-start | bytes 1048576
  93.3 8.9 %collective-permute-start.2 = (bf16[1,1,16,16,128]{4,0,3,2,1:T(2,128)(2,1)S(1)}, bf16[1,1,16,16,128]{4,0,3,2,1:T(2,128)(2,1)S(1)}, u32[]{:S(2)}, u32[]{:S(2)}) collective-permute-start(bf16[1,1,16,16,128]{4,0,3,2,1:T(2,128)(2,1)S(1)} %slice.84), channel_id=1, source_target_pairs={{1,0},{2,1},{3,2},{4,3},{5,4},{6,5},{7,6},{8,7},{9,8},{10,9},{11,1... | collective-permute-start | bytes 196616 | tf_op jit(solution)/shard_map/ppermute | solution.py:18
  114.2 389.0 %copy-start.2 = (bf16[1728,128]{1,0:T(8,128)(2,1)S(1)}, bf16[1728,128]{1,0:T(8,128)(2,1)}, u32[]{:S(2)}) copy-start(bf16[1728,128]{1,0:T(8,128)(2,1)} %copy-done.1) | copy-start | bytes 1327108
  114.2 389.0 %copy-start.6 = (pred[8,6]{0,1:T(8,128)(4,1)S(1)}, pred[8,6]{0,1:T(8,128)(4,1)}, u32[]{:S(2)}) copy-start(pred[8,6]{0,1:T(8,128)(4,1)} %constant.36) | copy-start | bytes 148
  502.1 68.1 %reduce-scatter.5.cloned.1.call-start = ((), (), s32[]{:S(2)}) async-start(), calls=%async_computation.4 | async-start | bytes 2211840 | tf_op jit(solution)/shard_map/reduce_scatter | solution.py:111
  503.2 6.2 %copy-start.3 = (bf16[2,8,8,2,256]{4,2,3,1,0:T(8,128)(2,1)S(1)}, bf16[2,8,8,2,256]{4,2,3,1,0:T(8,128)(2,1)}, u32[]{:S(2)}) copy-start(bf16[2,8,8,2,256]{4,2,3,1,0:T(8,128)(2,1)} %get-tuple-element.9) | copy-start | bytes 393220
  507.5 10.1 %collective-permute-start.3 = (bf16[1,1,32,32,64]{4,2,3,1,0:T(8,128)(2,1)}, bf16[1,1,32,32,64]{4,2,3,1,0:T(8,128)(2,1)}, u32[]{:S(2)}, u32[]{:S(2)}) collective-permute-start(bf16[1,1,32,32,64]{4,2,3,1,0:T(8,128)(2,1)} %slice_bitcast_fusion.1), channel_id=1, source_target_pairs={{1,0},{2,1},{3,2},{4,3},{5,4},{6,5},{7,6},{8,7},{9,8},{10,9},{11,1... | collective-permute-start | bytes 393224 | tf_op jit(solution)/shard_map/ppermute | solution.py:18
Sparse Core Ops, SparseCore 0:
  9.8 43.9 all-gather.1
  502.2 35.9 reduce-scatter.2
  540.8 29.3 reduce-scatter.4
where the time goes:
time: 590 us; the launch traced here: 579 us
  blocking collectives  416 us (71%)
  waiting for transfers between devices  63.2 us (11%)
  local copies, waits for them, and re-layouts  36.7 us (6%)
  matrix products  27.6 us (5%)
  between operations  14.5 us (2%)
  starting transfers between devices  14.1 us (2%)
  other arithmetic  6.55 us (1%)
    psum x1, blocking collectives, local(): summed = lax.psum((tally_first, tally_second), 'space')  388 us
    reduce_scatter x1, waiting for transfers between devices, local(): lax.psum_scatter(summed[1].astype(jnp.bfloat16), 'dp', scatter_dimension=...  30.4 us
    all_gather x1, blocking collectives, local(): lax.all_gather(weight_first, 'dp', axis=0, tiled=True)  28.4 us
    reduce_scatter x1, waiting for transfers between devices, local(): lax.psum_scatter(summed[0].astype(jnp.bfloat16), 'dp', scatter_dimension=...  18.2 us
    transpose x2, matrix products, kernel_gradient(): jnp.transpose(tapped, (1, 2, 3, 0, 4)).reshape(27 * channels, features)  14.6 us
    ppermute x4, starting transfers between devices, shifted(): return lax.ppermute(x, axis, pairs)  14 us
    ppermute x4, waiting for transfers between devices, shifted(): return lax.ppermute(x, axis, pairs)  13.2 us
  transfers between devices with their start and end apart: 7, of which 4 were waited for; matrix products, arithmetic and copies ran while one was open for 9% of the time, Pallas kernels for 0%

commit v1 on v0

v1 whole, which is shorter than its diff:
```python
import numpy as np

import jax
import jax.numpy as jnp
from jax import lax
from jax.experimental import pallas as pl
from jax.experimental.pallas import tpu as pltpu
from jax.sharding import PartitionSpec as P

NY, NZ = 4, 8
BF, F32 = jnp.bfloat16, jnp.float32
R1ROWS, R2ROWS = 512, 2048
MESH = pl.DeviceIdType.MESH


def rank_of(p):
    return (p % 2) * 8 + p // 2


def selections():
    spread = np.zeros((48, 32), np.float32)
    shift = np.zeros((16, 16), np.float32)
    merge = np.zeros((32, 32), np.float32)
    for p in range(16):
        for e in range(3):
            if 2 * p - 1 + e >= 0:
                spread[e * 16 + rank_of(p), 2 * p - 1 + e] = 1
        if p < 15:
            shift[rank_of(p), rank_of(p + 1)] = 1
        for parity in range(2):
            merge[2 * p + parity, parity * 16 + rank_of(p)] = 1
    taps = np.zeros((3, 3, 8, 8, 16, 16), np.float32)
    moved = np.zeros((2, 2, 8, 8, 8, 8), np.float32)
    for p in range(8):
        for q in range(8):
            for e in range(3):
                for f in range(3):
                    j, l = 2 * p - 1 + e, 2 * q - 1 + f
                    if j >= 0 and l >= 0:
                        taps[e, f, q, p, l, rank_of(j)] = 1
            for a in range(2):
                for b in range(2):
                    if q + a < 8 and p + b < 8:
                        moved[a, b, q, p, q + a, p + b] = 1
    return tuple(
        m.astype(BF)
        for m in (
            np.kron(np.eye(8), spread),
            taps.reshape(576, 256),
            moved.reshape(256, 64),
            np.kron(np.eye(16), shift),
            np.kron(np.eye(8), merge),
        )
    )


def place():
    d, s = lax.axis_index("dp"), lax.axis_index("space")
    return d // 2, d % 2, s // (2 * NZ), (s // 2) % NZ, s % 2


def device(xl, core, y, z, xh):
    return {"dp": xl * 2 + core, "space": (y * NZ + z) * 2 + xh}


def remote(src, dst, sems, slot, target):
    copy = pltpu.make_async_remote_copy(
        src_ref=src,
        dst_ref=dst,
        send_sem=sems.at[0, slot],
        recv_sem=sems.at[1, slot],
        device_id=target,
        device_id_type=MESH,
    )
    copy.start()
    return copy


def dot(a, b, ca=1, cb=0):
    return lax.dot_general(a, b, (((ca,), (cb,)), ((), ())), preferred_element_type=F32)


def act_and_slope(v):
    t = jnp.exp(-jnp.abs(v))
    soft = jnp.maximum(v, 0.0) + jnp.log(1.0 + t)
    gate = jnp.where(v >= 0, 1.0, t) / (1.0 + t)
    return 0.2 * v + 0.8 * soft, 0.2 + 0.8 * gate


def far_first(n):
    return sorted(range(1, n), key=lambda k: -min(k, n - k))


class Reduction:
    def __init__(self, rows, s, bufs, sems, peers):
        self.rows, self.s, self.sems, self.peers = rows, s, sems, peers
        self.r1, self.hy, self.r2, self.hz, self.r3, self.kx, self.r4, self.g = bufs
        self.copies = []
        self.slot = 0
        self.at = place()

    def send(self, src, dst, target):
        copy = remote(src, dst, self.sems, self.slot, target)
        self.slot += 1
        self.copies.append(copy)
        return copy

    def cores(self):
        xl, core, y, z, xh = self.at
        self.order = sorted(range(1, NY), key=lambda k: min(k, NY - k)) + [0]
        self.first = {}
        for k in self.order:
            there = (y + k) % NY
            for h in range(2):
                self.first[k, h] = self.send(
                    self.s.at[h * 2 + 1 - core, pl.ds(there * NZ, NZ)], self.r1.at[k, h], self.peers["core"]
                )

    def along_y(self):
        xl, core, y, z, xh = self.at
        self.second = []
        for k in self.order:
            there = (y + k) % NY
            for h in range(2):
                self.first[k, h].wait_recv()

                @pl.loop(0, NZ)
                def _(i, h=h, k=k, there=there):
                    mine = self.s[h * 2 + core, there * NZ + i].astype(F32)
                    self.hy[k, h, i] = (mine + self.r1[k, h, i].astype(F32)).astype(BF)

            if k:
                self.second.append(self.send(self.hy.at[k], self.r2.at[k - 1], self.peers["y", k]))

    def along_z(self):
        xl, core, y, z, xh = self.at
        for copy in self.second:
            copy.wait_recv()
        self.third = []
        for k in far_first(NZ) + [0]:
            there = (z + k) % NZ
            for h in range(2):
                total = self.hy[0, h, there].astype(F32)
                for j in range(NY - 1):
                    total += self.r2[j, h, there].astype(F32)
                self.hz[k, h] = total.astype(BF)
            if k:
                self.third.append(self.send(self.hz.at[k], self.r3.at[k - 1], self.peers["z", k]))

    def along_x(self):
        xl, core, y, z, xh = self.at
        for copy in self.third:
            copy.wait_recv()
        for h in range(2):
            total = self.hz[0, h].astype(F32)
            for j in range(NZ - 1):
                total += self.r3[j, h].astype(F32)
            self.kx[h] = total.astype(BF)
        self.fourth = []
        for j, half in enumerate((1 - xl, xl, 1 - xl)):
            self.fourth.append(self.send(self.kx.at[half], self.r4.at[j], self.peers["x", j]))

    def gather_z(self):
        xl, core, y, z, xh = self.at
        total = self.kx[xl].astype(F32)
        for j, copy in enumerate(self.fourth):
            copy.wait_recv()
            total += self.r4[j].astype(F32)
        self.g[y, z] = total.astype(BF)
        self.fifth = []
        for k in far_first(NZ):
            self.fifth.append(self.send(self.g.at[y, z], self.g.at[y, z], self.peers["z", k]))

    def gather_y(self):
        xl, core, y, z, xh = self.at
        for copy in self.fifth:
            copy.wait_recv()
        self.sixth = []
        for k in far_first(NY):
            self.sixth.append(self.send(self.g.at[y], self.g.at[y], self.peers["y", k]))

    def finish(self):
        for copy in self.sixth:
            copy.wait_recv()

    def drain(self):
        for copy in self.copies:
            copy.wait_send()

    @staticmethod
    def scratch(rows):
        piece = rows // (NY * NZ)
        return [
            pltpu.VMEM((4, NY * NZ, piece, 128), BF),
            pltpu.VMEM((NY, 2, NZ, piece, 128), BF),
            pltpu.VMEM((NY, 2, NZ, piece, 128), BF),
            pltpu.VMEM((max(NY - 1, 1), 2, NZ, piece, 128), BF),
            pltpu.VMEM((NZ, 2, piece, 128), BF),
            pltpu.VMEM((NZ - 1, 2, piece, 128), BF),
            pltpu.VMEM((2, piece, 128), BF),
            pltpu.VMEM((3, piece, 128), BF),
            pltpu.VMEM((NY, NZ, piece, 128), BF),
            pltpu.SemaphoreType.DMA((2, 2 * NY + 2 * (NY - 1) + 2 * (NZ - 1) + 3)),
        ]


def step_kernel(scales, vol, w1, w2, cot, p0, p1, p2, p3, p4, actv, ig, g1out, g2out, *scratch):
    xe, xhalo, w1g, w1p, wb, w2g, hid, hhalo, slope, l2, d2, d2e, d1e, un = scratch[:14]
    wsem, hsem = scratch[14:16]
    s1, *bufs1, sems1 = scratch[16:26]
    s2, *bufs2, sems2 = scratch[26:36]
    at = xl, core, y, z, xh = place()
    s, d = lax.axis_index("space"), lax.axis_index("dp")
    n = 2 * NY * NZ
    bottom, top = s == 0, s == n - 1
    upper = {"space": (s + 1) % n}
    lower = {"space": (s + n - 1) % n}
    peers = {"core": device(xl, 1 - core, y, z, xh)}
    for k in range(1, NY):
        peers["y", k] = device(xl, core, (y + k) % NY, z, xh)
    for k in range(1, NZ):
        peers["z", k] = device(xl, core, y, (z + k) % NZ, xh)
    peers["x", 0] = device(1 - xl, core, y, z, xh)
    peers["x", 1] = device(xl, core, y, z, 1 - xh)
    peers["x", 2] = device(1 - xl, core, y, z, 1 - xh)
    peers["upper"], peers["lower"] = upper, lower

    barrier = pltpu.get_barrier_semaphore()
    for peer in peers.values():
        pl.semaphore_signal(barrier, inc=1, device_id=peer, device_id_type=MESH)
    pl.semaphore_wait(barrier, len(peers))

    def rows(q, size, lo, hi):
        return pl.ds(pl.multiple_of(q * size + lo, 16), hi - lo)

    sent = []
    forward = []
    theirs = (1 - xl) * 2 + core
    for slot, (own, whole, size, cut) in enumerate(((w1, w1g, 432, 224), (w2, w2g, 864, 432))):
        base = slot * 5
        parts = ((0, cut, peers["x", 0]), (cut, size, peers["x", 2]))
        arriving = []
        for j, (lo, hi, peer) in enumerate(parts):
            arriving.append(remote(own.at[pl.ds(lo, hi - lo)], whole.at[rows(d, size, lo, hi)], wsem, base + j, peer))
        to_core = remote(own, whole.at[rows(d, size, 0, size)], wsem, base + 2, peers["core"])
        forward.append((whole, size, parts, arriving, to_core, base))
        sent += arriving + [to_core]
        if slot == 0:
            halo_in = remote(vol.at[pl.ds(224, 32)], xhalo, hsem, 0, upper)

    passed = []

    def pass_on(slot):
        whole, size, parts, arriving, to_core, base = forward[slot]
        for j, (lo, hi, _) in enumerate(parts):
            arriving[j].wait_recv()
            part = whole.at[rows(theirs, size, lo, hi)]
            passed.append(remote(part, part, wsem, base + 3 + j, peers["core"]))
        return to_core, passed[-2:]

    xe[:, :, 0] = jnp.zeros((9, 3, 16, 128), BF)

    @pl.loop(0, 8)
    def _(c):
        got = dot(p0[...], vol[:, pl.ds(pl.multiple_of(c * 256, 256), 256)]).astype(BF)
        for i in range(8):
            for e in range(3):
                for u in range(2):
                    xe[i + 1, e, 2 * c + 1 + u] = got[(i * 3 + e) * 16 : (i * 3 + e + 1) * 16, u * 128 : (u + 1) * 128]

    w1g[rows(d, 432, 0, 432)] = w1[...]
    w2g[rows(d, 864, 0, 864)] = w2[...]
    to_core, others = pass_on(0)
    to_core.wait_recv()
    for copy in others:
        copy.wait_recv()
    for t in range(9):
        w1p[t * 256 : t * 256 + 64] = jnp.zeros((64, 128), BF)
        w1p[t * 256 + 64 : t * 256 + 256] = w1g[t * 192 : (t + 1) * 192]

    def conv_first(o):
        tiles = []
        for a in range(3):
            for e in range(3):
                tiles.append(xe[2 * o + a, e, 0:16].reshape(256, 128))
                tiles.append(xe[2 * o + a, e, 1:17].reshape(256, 128))
        value, gate = act_and_slope(dot(jnp.concatenate(tiles, axis=1), w1p[...]))
        hid[o] = value.astype(BF)
        slope[o] = gate.reshape(16, 16, 128)

    conv_first(3)
    halo_hid = remote(hid.at[3], hhalo, hsem, 1, upper)
    to_core_second, others_second = pass_on(1)

    @pl.loop(1, 3)
    def _(o):
        conv_first(o)

    halo_in.wait_recv()
    rim = jnp.where(bottom, jnp.zeros_like(xhalo), xhalo[...])
    got = dot(p0[0:48, 0:32], rim).astype(BF)
    for e in range(3):
        for u in range(16):
            xe[0, e, u + 1] = got[e * 16 : (e + 1) * 16, u * 128 : (u + 1) * 128]
    conv_first(0)

    def place_taps(got, plane):
        for o in range(2):
            a = plane - 2 * o
            if 0 <= a < 3:
                for k in range(9):
                    l2[o * 64 : (o + 1) * 64, (a * 9 + k) * 128 : (a * 9 + k + 1) * 128] = got[k * 64 : (k + 1) * 64]

    for pair in range(2):
        both = jnp.concatenate([hid[2 * pair], hid[2 * pair + 1]], axis=1)
        got = dot(p1[...], both).astype(BF)
        place_taps(got[:, :128], 2 * pair + 1)
        place_taps(got[:, 128:], 2 * pair + 2)
    for t in range(9):
        block = w1p[t * 256 : (t + 1) * 256]
        wb[t * 256 : t * 256 + 128] = block[128:].T
        wb[t * 256 + 128 : (t + 1) * 256] = block[:128].T
    halo_hid.wait_recv()
    rim = jnp.where(bottom, jnp.zeros_like(hhalo), hhalo[...])
    place_taps(dot(p1[...], rim).astype(BF), 0)
    to_core_second.wait_recv()
    for copy in others_second:
        copy.wait_recv()

    linear = dot(l2[...], w2g[...])
    value, gate = act_and_slope(linear)
    arriving = jnp.concatenate(
        [cot[o, :, q * 256 : (q + 1) * 256].astype(F32) for o in range(2) for q in range(8)], axis=0
    )
    delta = (arriving * gate).astype(BF)
    d2[0] = delta[:64]
    halo_d2 = remote(d2.at[0], d2.at[2], hsem, 2, lower)
    d2[1] = delta[64:]
    for o in range(2):
        for q in range(8):
            at_row = (o * 8 + q) * 8
            actv[o, :, q * 256 : (q + 1) * 256] = value[at_row : at_row + 8].astype(BF)

    piece1, piece2 = R1ROWS // (NY * NZ), R2ROWS // (NY * NZ)
    s2[:, 1728 // piece2 :] = jnp.zeros((4, NY * NZ - 1728 // piece2, piece2, 128), BF)
    s1[:, 432 // piece1 :] = jnp.zeros((4, NY * NZ - 432 // piece1, piece1, 128), BF)
    for t in range(27):
        got = dot(l2[:, t * 128 : (t + 1) * 128], delta, 0, 0).astype(BF)
        for k in range(4):
            row = t * 128 + 32 * k
            for half in range(2):
                flat = half * 864 + row % 864
                s2[row // 864, flat // piece2, flat % piece2 : flat % piece2 + 32] = got[
                    32 * k : 32 * k + 32, half * 128 : (half + 1) * 128
                ]
    sum2 = Reduction(R2ROWS, s2, bufs2, sems2, peers)
    sum1 = Reduction(R1ROWS, s1, bufs1, sems1, peers)
    sum2.cores()

    def spread_delta(o):
        got = dot(p2[...], d2[o]).astype(BF)
        for v in range(4):
            d2e[o, v] = got[v * 64 : (v + 1) * 64]

    taps_of = (((1, 0),), ((2, 0), (0, 1)))

    def hidden_delta(pi):
        for pq in range(2):
            halves = []
            for pj in range(2):
                left, right = [], []
                for a, sa in taps_of[pi]:
                    for e, se in taps_of[pj]:
                        for f, sf in taps_of[pq]:
                            left.append(d2e[sa : sa + 2, sf * 2 + se].reshape(128, 256))
                            t = a * 9 + e * 3 + f
                            right.append(w2g[t * 128 : (t + 1) * 128])
                got = dot(jnp.concatenate(left, axis=1), jnp.concatenate(right, axis=1), 1, 1)
                halves.append(got.reshape(2, 8, 8, 128))
            both = jnp.concatenate(halves, axis=2)
            for i in range(2):
                for q in range(8):
                    d1e[2 * i + pi, 0, 2 * q + pq] = (both[i, q] * slope[2 * i + pi, 2 * q + pq]).astype(BF)

    spread_delta(0)
    spread_delta(1)
    d1e[:, :, 16] = jnp.zeros((5, 2, 16, 128), BF)
    hidden_delta(0)
    halo_d1 = remote(d1e.at[0, 0, pl.ds(0, 16)], d1e.at[4, 0, pl.ds(0, 16)], hsem, 3, lower)
    sum2.along_y()
    halo_d2.wait_recv()
    d2[2] = jnp.where(top, jnp.zeros((64, 256), BF), d2[2])
    spread_delta(2)
    hidden_delta(1)

    flat1 = jnp.concatenate([d1e[o, 0, 0:16].reshape(256, 128) for o in range(4)], axis=0)

    @pl.loop(0, 9)
    def _(t):
        a, e = t // 3, t % 3
        left = jnp.concatenate(
            [
                jnp.concatenate(
                    [xe[2 * o + a, e, 0:16].reshape(256, 128), xe[2 * o + a, e, 1:17].reshape(256, 128)], axis=1
                )
                for o in range(4)
            ],
            axis=0,
        )
        got = dot(left, flat1, 0, 0).astype(BF)
        for k in range(12):
            block = t * 12 + k
            row = (block % 27) * 16
            s1[block // 27, row // piece1, pl.ds(pl.multiple_of(row % piece1, 16), 16)] = got[
                64 + k * 16 : 64 + (k + 1) * 16
            ]

    sum1.cores()
    sum2.along_z()

    def shift_delta(first, count):
        both = jnp.concatenate([d1e[first + k, 0, 0:16].reshape(256, 128) for k in range(count)], axis=1)
        got = dot(p3[...], both).astype(BF)
        for k in range(count):
            d1e[first + k, 1, 0:16] = got[:, k * 128 : (k + 1) * 128].reshape(16, 16, 128)

    def input_delta(pi, pj):
        @pl.loop(0, 4)
        def _(i):
            left, right = [], []
            for a, sa in taps_of[pi]:
                for e, se in taps_of[pj]:
                    left.append(d1e[i + sa, se, 0:16].reshape(256, 128))
                    left.append(d1e[i + sa, se, 1:17].reshape(256, 128))
                    t = a * 3 + e
                    right.append(wb[t * 256 : (t + 1) * 256])
            got = dot(jnp.concatenate(left, axis=1), jnp.concatenate(right, axis=0)).astype(BF)
            for q in range(16):
                un[2 * i + pi, pj * 16 : (pj + 1) * 16, q * 128 : (q + 1) * 128] = got[q * 16 : (q + 1) * 16]

    shift_delta(0, 2)
    shift_delta(2, 2)
    sum1.along_y()
    input_delta(0, 0)
    sum2.along_x()
    input_delta(0, 1)
    sum1.along_z()
    sum2.gather_z()
    halo_d1.wait_recv()
    d1e[4, 0, 0:16] = jnp.where(top, jnp.zeros((16, 16, 128), BF), d1e[4, 0, 0:16])
    shift_delta(4, 1)
    input_delta(1, 0)
    sum1.along_x()
    sum2.gather_y()
    input_delta(1, 1)
    sum1.gather_z()

    @pl.loop(0, 8)
    def _(c):
        lanes = pl.ds(pl.multiple_of(c * 256, 256), 256)
        ig[:, lanes] = dot(p4[...], un[:, :, lanes].reshape(256, 256)).astype(BF)

    sum1.gather_y()
    sum2.finish()
    whole = bufs2[-1]
    for block in range(54):
        flat = block * 32
        k = flat // piece2
        got = whole[k // NZ, k % NZ, flat % piece2 : flat % piece2 + 32].astype(F32) * scales[1]
        g2out[flat % 864 : flat % 864 + 32, flat // 864 * 128 : (flat // 864 + 1) * 128] = got
    sum1.finish()
    whole = bufs1[-1]
    for block in range(27):
        flat = block * 16
        k = flat // piece1
        g1out[flat : flat + 16] = whole[k // NZ, k % NZ, flat % piece1 : flat % piece1 + 16].astype(F32) * scales[0]

    for copy in sent + passed + [halo_in, halo_hid, halo_d2, halo_d1]:
        copy.wait_send()
    sum2.drain()
    sum1.drain()


def local(volume, weight_first, weight_second, cotangent):
    cells = 4 * lax.axis_size("space") * 4 * 256
    scales = (float(cells) ** -0.5, float(cells // 8) ** -0.5)
    vmem = pl.BlockSpec(memory_space=pltpu.VMEM)
    shape = jax.ShapeDtypeStruct

    def body(*refs):
        step_kernel(scales, *refs)

    activations, input_gradient, first, second = pl.pallas_call(
        body,
        out_shape=(
            shape((2, 8, 2048), BF),
            shape((256, 2048), BF),
            shape((432, 128), F32),
            shape((864, 256), F32),
        ),
        in_specs=[vmem] * 9,
        out_specs=(vmem,) * 4,
        scratch_shapes=[
            pltpu.VMEM((9, 3, 17, 16, 128), BF),
            pltpu.VMEM((32, 2048), BF),
            pltpu.VMEM((1728, 128), BF),
            pltpu.VMEM((2304, 128), BF),
            pltpu.VMEM((2304, 128), BF),
            pltpu.VMEM((3456, 256), BF),
            pltpu.VMEM((4, 256, 128), BF),
            pltpu.VMEM((256, 128), BF),
            pltpu.VMEM((4, 16, 16, 128), F32),
            pltpu.VMEM((128, 3456), BF),
            pltpu.VMEM((3, 64, 256), BF),
            pltpu.VMEM((3, 4, 64, 256), BF),
            pltpu.VMEM((5, 2, 17, 16, 128), BF),
            pltpu.VMEM((8, 32, 2048), BF),
            pltpu.SemaphoreType.DMA((2, 10)),
            pltpu.SemaphoreType.DMA((2, 4)),
        ]
        + Reduction.scratch(R1ROWS)
        + Reduction.scratch(R2ROWS),
        compiler_params=pltpu.CompilerParams(
            collective_id=0, has_side_effects=True, vmem_limit_bytes=60 * 1024 * 1024
        ),
        name="step",
    )(
        volume.reshape(256, 2048),
        weight_first,
        weight_second,
        cotangent.reshape(2, 8, 2048),
        *selections(),
    )
    return (
        activations.reshape(cotangent.shape),
        input_gradient.reshape(volume.shape),
        first,
        second,
    )


def solution(mesh):
    return jax.shard_map(
        local,
        mesh=mesh,
        in_specs=(
            P("dp", "space", None, None),
            P("dp", None),
            P("dp", None),
            P("dp", "space", None, None),
        ),
        out_specs=(
            P("dp", "space", None, None),
            P("dp", "space", None, None),
            P("dp", None),
            P("dp", None),
        ),
        check_vma=False,
    )
```

time: 590 us -> 76.6 us (0.13); the launches traced: 579 us -> 76.3 us
  blocking collectives: 416 us -> 0 us
  Pallas kernels: 0 us -> 70.2 us
  waiting for transfers between devices: 63.2 us -> 0 us
  local copies, waits for them, and re-layouts: 36.7 us -> 5.47 us
  matrix products: 27.6 us -> 0 us
  starting transfers between devices: 14.1 us -> 0 us
  between operations: 14.5 us -> 0.64 us
  other arithmetic: 6.55 us -> 0 us
    psum x1 -> x0, blocking collectives: 388 us -> none  [local(): summed = lax.psum((tally_first, tally_second), 'space')]
    pallas_call x0 -> x1, Pallas kernels: none -> 70.2 us  [local(): pl.pallas_call(body, out_shape=(shape((2, 8, 2048), BF), shape((256, 2048...]
    reduce_scatter x2 -> x0, waiting for transfers between devices: 48.6 us -> none  [the longest x1 30.4 us: local(): lax.psum_scatter(summed[1].astype(jnp.bfloat16), 'dp', scatter_dimension=...]
    all_gather x1 -> x0, blocking collectives: 28.4 us -> none  [local(): lax.all_gather(weight_first, 'dp', axis=0, tiled=True)]
    transpose x2 -> x0, matrix products: 14.6 us -> none  [kernel_gradient(): jnp.transpose(tapped, (1, 2, 3, 0, 4)).reshape(27 * channels, features)]
    ppermute x4 -> x0, starting transfers between devices: 14 us -> none  [shifted(): return lax.ppermute(x, axis, pairs)]
    ppermute x4 -> x0, waiting for transfers between devices: 13.2 us -> none  [shifted(): return lax.ppermute(x, axis, pairs)]
    conv_general_dilated x4 -> x0, matrix products: 13 us -> none  [the longest x2 7.55 us: convolve_back(): lax.conv_general_dilated(delta, flipped, (1, 1, 1), ((2, 2), (1, 2), (1,...]
  transfers between devices with their start and end apart: 7 -> 0, of which waited for: 4 -> 0; matrix products, arithmetic and copies ran while one was open for 9% -> 0% of each run, Pallas kernels for 0% -> 0%
where the time goes in v1:
time: 76.6 us; the launch traced here: 76.3 us
  Pallas kernels  70.2 us (92%)
  local copies, waits for them, and re-layouts  5.47 us (7%)
    pallas_call x1, Pallas kernels, local(): pl.pallas_call(body, out_shape=(shape((2, 8, 2048), BF), shape((256, 2048...  70.2 us
    unnamed x8, local copies, waits for them, and re-layouts  5.47 us

profile of v1, /device:TPU:8, one launch (start us, length us, event | category | flops | bytes accessed | tf_op | source)
XLA Modules:
  0.0 76.3 jit_solution(4313916327169852882)
XLA Ops:
  0.6 70.2 %step.1 = (bf16[2,8,2048]{2,1,0:T(8,128)(2,1)}, bf16[256,2048]{1,0:T(8,128)(2,1)}, f32[432,128]{1,0:T(8,128)}, f32[864,256]{1,0:T(8,128)}) custom-call(bf16[256,2048]{1,0:T(8,128)(2,1)} %bitcast.4, bf16[432,128]{1,0:T(8,128)(2,1)} %refs_1_.1, bf16[864,256]{1,0:T(8,128)(2,1)} %refs_2_.1, bf16[2,8,2048]{2,1,0:T(8,128)(2,1)} %bitcast.6, ...), custom_call_target="tpu_custom_call" | custom-call | tf_op jit(solution)/shard_map/step/pallas_call | solution.py:493
  70.8 1.5 %copy.17 = bf16[1,2,8,2048]{3,2,1,0:T(8,128)(2,1)} copy(bf16[1,2,8,2048]{3,2,1,0:T(8,128)(2,1)} %bitcast.7) | data formatting | bytes 131072
  72.3 0.0 copy-start.1
  72.3 0.0 copy-start
  72.3 2.4 %copy.18 = bf16[1,8,32,2048]{3,2,1,0:T(8,128)(2,1)} copy(bf16[1,8,32,2048]{3,2,1,0:T(8,128)(2,1)} %bitcast.5) | data formatting | bytes 2097152
  74.7 0.0 copy-done.1
  74.7 0.7 copy.19
  75.4 0.0 copy-done
  75.4 0.9 %copy.20 = f32[864,256]{1,0:T(8,128)} copy(f32[864,256]{1,0:T(8,128)S(1)} %copy-done) | data formatting | bytes 1769472
Async XLA Ops:
  72.3 2.4 %copy-start.1 = (f32[432,128]{1,0:T(8,128)S(1)}, f32[432,128]{1,0:T(8,128)}, u32[]{:S(2)}) copy-start(f32[432,128]{1,0:T(8,128)} %get-tuple-element.18) | copy-start | bytes 663556
  72.3 3.1 %copy-start = (f32[864,256]{1,0:T(8,128)S(1)}, f32[864,256]{1,0:T(8,128)}, u32[]{:S(2)}) copy-start(f32[864,256]{1,0:T(8,128)} %get-tuple-element.19) | copy-start | bytes 2654212

commit v2 on v1

--- a/solution.py
+++ b/solution.py
@@ -9,7 +9,9 @@
 
 NY, NZ = 4, 8
 BF, F32 = jnp.bfloat16, jnp.float32
-R1ROWS, R2ROWS = 512, 2048
+PIECE1, PIECE2 = 8, 32
+GROUP1, GROUP2 = 56, 216
+USED = 7
 MESH = pl.DeviceIdType.MESH
 
 
@@ -92,9 +94,9 @@
 
 
 class Reduction:
-    def __init__(self, rows, s, bufs, sems, peers):
-        self.rows, self.s, self.sems, self.peers = rows, s, sems, peers
-        self.r1, self.hy, self.r2, self.hz, self.r3, self.kx, self.r4, self.g = bufs
+    def __init__(self, s, bufs, sems, peers):
+        self.s, self.sems, self.peers = s, sems, peers
+        self.r1, self.hy, self.r2, self.hz, self.r3, self.g = bufs
         self.copies = []
         self.slot = 0
         self.at = place()
@@ -107,30 +109,39 @@
 
     def cores(self):
         xl, core, y, z, xh = self.at
-        self.order = sorted(range(1, NY), key=lambda k: min(k, NY - k)) + [0]
+        self.order = far_first(NY) + [0]
         self.first = {}
         for k in self.order:
             there = (y + k) % NY
             for h in range(2):
                 self.first[k, h] = self.send(
-                    self.s.at[h * 2 + 1 - core, pl.ds(there * NZ, NZ)], self.r1.at[k, h], self.peers["core"]
+                    self.s.at[h * 2 + 1 - core, there, :, pl.ds(0, USED)],
+                    self.r1.at[k, h, :, pl.ds(0, USED)],
+                    self.peers["core"],
                 )
 
-    def along_y(self):
+    def plane(self):
         xl, core, y, z, xh = self.at
         self.second = []
         for k in self.order:
             there = (y + k) % NY
             for h in range(2):
                 self.first[k, h].wait_recv()
-
-                @pl.loop(0, NZ)
-                def _(i, h=h, k=k, there=there):
-                    mine = self.s[h * 2 + core, there * NZ + i].astype(F32)
-                    self.hy[k, h, i] = (mine + self.r1[k, h, i].astype(F32)).astype(BF)
-
-            if k:
-                self.second.append(self.send(self.hy.at[k], self.r2.at[k - 1], self.peers["y", k]))
+            for h in range(2):
+                for v in range(2):
+                    left = xl + h - 2 * xl * h
+                    half = xh + v - 2 * xh * v
+                    for i in range(USED):
+                        mine = self.s[left * 2 + core, there, half, i].astype(F32)
+                        self.hy[k, h, v, i] = (mine + self.r1[k, left, half, i].astype(F32)).astype(BF)
+                    if (k, h, v) != (0, 0, 0):
+                        self.second.append(
+                            self.send(
+                                self.hy.at[k, h, v, pl.ds(0, USED)],
+                                self.r2.at[k, h, v, pl.ds(0, USED)],
+                                self.peers["plane", k, h, v],
+                            )
+                        )
 
     def along_z(self):
         xl, core, y, z, xh = self.at
@@ -139,45 +150,38 @@
         self.third = []
         for k in far_first(NZ) + [0]:
             there = (z + k) % NZ
-            for h in range(2):
-                total = self.hy[0, h, there].astype(F32)
-                for j in range(NY - 1):
-                    total += self.r2[j, h, there].astype(F32)
-                self.hz[k, h] = total.astype(BF)
+            total = self.hy[0, 0, 0, there].astype(F32)
+            for j in range(NY):
+                for h in range(2):
+                    for v in range(2):
+                        if (j, h, v) != (0, 0, 0):
+                            total += self.r2[j, h, v, there].astype(F32)
+            self.hz[k] = total.astype(BF)
             if k:
                 self.third.append(self.send(self.hz.at[k], self.r3.at[k - 1], self.peers["z", k]))
 
-    def along_x(self):
+    def gather_z(self):
         xl, core, y, z, xh = self.at
         for copy in self.third:
             copy.wait_recv()
-        for h in range(2):
-            total = self.hz[0, h].astype(F32)
-            for j in range(NZ - 1):
-                total += self.r3[j, h].astype(F32)
-            self.kx[h] = total.astype(BF)
-        self.fourth = []
-        for j, half in enumerate((1 - xl, xl, 1 - xl)):
-            self.fourth.append(self.send(self.kx.at[half], self.r4.at[j], self.peers["x", j]))
-
-    def gather_z(self):
-        xl, core, y, z, xh = self.at
-        total = self.kx[xl].astype(F32)
-        for j, copy in enumerate(self.fourth):
-            copy.wait_recv()
-            total += self.r4[j].astype(F32)
-        self.g[y, z] = total.astype(BF)
+        total = self.hz[0].astype(F32)
+        for j in range(NZ - 1):
+            total += self.r3[j].astype(F32)
+        self.g[y, xh, z] = total.astype(BF)
         self.fifth = []
         for k in far_first(NZ):
-            self.fifth.append(self.send(self.g.at[y, z], self.g.at[y, z], self.peers["z", k]))
-
-    def gather_y(self):
+            self.fifth.append(self.send(self.g.at[y, xh, z], self.g.at[y, xh, z], self.peers["z", k]))
+
+    def gather_plane(self):
         xl, core, y, z, xh = self.at
         for copy in self.fifth:
             copy.wait_recv()
         self.sixth = []
-        for k in far_first(NY):
-            self.sixth.append(self.send(self.g.at[y], self.g.at[y], self.peers["y", k]))
+        part = self.g.at[y, xh, pl.ds(0, USED)]
+        for k in far_first(NY) + [0]:
+            for v in (1, 0):
+                if (k, v) != (0, 0):
+                    self.sixth.append(self.send(part, part, self.peers["plane", k, 0, v]))
 
     def finish(self):
         for copy in self.sixth:
@@ -188,27 +192,25 @@
             copy.wait_send()
 
     @staticmethod
-    def scratch(rows):
-        piece = rows // (NY * NZ)
+    def scratch(piece):
+        blocks = (NY, 2, 2, NZ, piece, 128)
         return [
-            pltpu.VMEM((4, NY * NZ, piece, 128), BF),
+            pltpu.VMEM((4, NY, 2, NZ, piece, 128), BF),
+            pltpu.VMEM(blocks, BF),
+            pltpu.VMEM(blocks, BF),
+            pltpu.VMEM(blocks, BF),
+            pltpu.VMEM((NZ, piece, 128), BF),
+            pltpu.VMEM((NZ - 1, piece, 128), BF),
             pltpu.VMEM((NY, 2, NZ, piece, 128), BF),
-            pltpu.VMEM((NY, 2, NZ, piece, 128), BF),
-            pltpu.VMEM((max(NY - 1, 1), 2, NZ, piece, 128), BF),
-            pltpu.VMEM((NZ, 2, piece, 128), BF),
-            pltpu.VMEM((NZ - 1, 2, piece, 128), BF),
-            pltpu.VMEM((2, piece, 128), BF),
-            pltpu.VMEM((3, piece, 128), BF),
-            pltpu.VMEM((NY, NZ, piece, 128), BF),
-            pltpu.SemaphoreType.DMA((2, 2 * NY + 2 * (NY - 1) + 2 * (NZ - 1) + 3)),
+            pltpu.SemaphoreType.DMA((2, 2 * NY + (4 * NY - 1) + 2 * (NZ - 1) + (2 * NY - 1))),
         ]
 
 
 def step_kernel(scales, vol, w1, w2, cot, p0, p1, p2, p3, p4, actv, ig, g1out, g2out, *scratch):
     xe, xhalo, w1g, w1p, wb, w2g, hid, hhalo, slope, l2, d2, d2e, d1e, un = scratch[:14]
     wsem, hsem = scratch[14:16]
-    s1, *bufs1, sems1 = scratch[16:26]
-    s2, *bufs2, sems2 = scratch[26:36]
+    s1, *bufs1, sems1 = scratch[16:24]
+    s2, *bufs2, sems2 = scratch[24:32]
     at = xl, core, y, z, xh = place()
     s, d = lax.axis_index("space"), lax.axis_index("dp")
     n = 2 * NY * NZ
@@ -216,13 +218,14 @@
     upper = {"space": (s + 1) % n}
     lower = {"space": (s + n - 1) % n}
     peers = {"core": device(xl, 1 - core, y, z, xh)}
-    for k in range(1, NY):
-        peers["y", k] = device(xl, core, (y + k) % NY, z, xh)
+    for k in range(NY):
+        for h in range(2):
+            for v in range(2):
+                if (k, h, v) != (0, 0, 0):
+                    there = xl + h - 2 * xl * h, core, (y + k) % NY, z, xh + v - 2 * xh * v
+                    peers["plane", k, h, v] = device(*there)
     for k in range(1, NZ):
         peers["z", k] = device(xl, core, y, (z + k) % NZ, xh)
-    peers["x", 0] = device(1 - xl, core, y, z, xh)
-    peers["x", 1] = device(xl, core, y, z, 1 - xh)
-    peers["x", 2] = device(1 - xl, core, y, z, 1 - xh)
     peers["upper"], peers["lower"] = upper, lower
 
     barrier = pltpu.get_barrier_semaphore()
@@ -238,7 +241,7 @@
     theirs = (1 - xl) * 2 + core
     for slot, (own, whole, size, cut) in enumerate(((w1, w1g, 432, 224), (w2, w2g, 864, 432))):
         base = slot * 5
-        parts = ((0, cut, peers["x", 0]), (cut, size, peers["x", 2]))
+        parts = ((0, cut, peers["plane", 0, 1, 0]), (cut, size, peers["plane", 0, 1, 1]))
         arriving = []
         for j, (lo, hi, peer) in enumerate(parts):
             arriving.append(remote(own.at[pl.ds(lo, hi - lo)], whole.at[rows(d, size, lo, hi)], wsem, base + j, peer))
@@ -341,20 +344,25 @@
             at_row = (o * 8 + q) * 8
             actv[o, :, q * 256 : (q + 1) * 256] = value[at_row : at_row + 8].astype(BF)
 
-    piece1, piece2 = R1ROWS // (NY * NZ), R2ROWS // (NY * NZ)
-    s2[:, 1728 // piece2 :] = jnp.zeros((4, NY * NZ - 1728 // piece2, piece2, 128), BF)
-    s1[:, 432 // piece1 :] = jnp.zeros((4, NY * NZ - 432 // piece1, piece1, 128), BF)
+    def pieces(lo, hi, group, piece):
+        while lo < hi:
+            where = lo % group
+            count = min(hi - lo, group - where, piece - where % piece)
+            yield lo, count, lo // group, where // piece, where % piece
+            lo += count
+
     for t in range(27):
-        got = dot(l2[:, t * 128 : (t + 1) * 128], delta, 0, 0).astype(BF)
-        for k in range(4):
-            row = t * 128 + 32 * k
-            for half in range(2):
-                flat = half * 864 + row % 864
-                s2[row // 864, flat // piece2, flat % piece2 : flat % piece2 + 32] = got[
-                    32 * k : 32 * k + 32, half * 128 : (half + 1) * 128
-                ]
-    sum2 = Reduction(R2ROWS, s2, bufs2, sems2, peers)
-    sum1 = Reduction(R1ROWS, s1, bufs1, sems1, peers)
+        got = dot(l2[:, t * 128 : (t + 1) * 128], delta, 0, 0)
+        for q in range(4):
+            lo, hi = max(t * 128, q * 864), min(t * 128 + 128, q * 864 + 864)
+            for row, count, g, k, at_row in pieces(lo - q * 864, hi - q * 864, GROUP2, PIECE2):
+                row += q * 864 - t * 128
+                for half in range(2):
+                    block = got[row : row + count, half * 128 : (half + 1) * 128].astype(BF)
+                    h = half * NY + g
+                    s2[q, h // 2, h % 2, k, at_row : at_row + count] = block
+    sum2 = Reduction(s2, bufs2, sems2, peers)
+    sum1 = Reduction(s1, bufs1, sems1, peers)
     sum2.cores()
 
     def spread_delta(o):
@@ -387,7 +395,7 @@
     d1e[:, :, 16] = jnp.zeros((5, 2, 16, 128), BF)
     hidden_delta(0)
     halo_d1 = remote(d1e.at[0, 0, pl.ds(0, 16)], d1e.at[4, 0, pl.ds(0, 16)], hsem, 3, lower)
-    sum2.along_y()
+    sum2.plane()
     halo_d2.wait_recv()
     d2[2] = jnp.where(top, jnp.zeros((64, 256), BF), d2[2])
     spread_delta(2)
@@ -407,13 +415,11 @@
             ],
             axis=0,
         )
-        got = dot(left, flat1, 0, 0).astype(BF)
-        for k in range(12):
-            block = t * 12 + k
-            row = (block % 27) * 16
-            s1[block // 27, row // piece1, pl.ds(pl.multiple_of(row % piece1, 16), 16)] = got[
-                64 + k * 16 : 64 + (k + 1) * 16
-            ]
+        got = dot(left, flat1, 0, 0)
+        for k in range(24):
+            block = t * 24 + k
+            g = block % 54 // 7
+            s1[block // 54, g // 2, g % 2, block % 54 % 7] = got[64 + k * 8 : 64 + (k + 1) * 8].astype(BF)
 
     sum1.cores()
     sum2.along_z()
@@ -440,9 +446,8 @@
 
     shift_delta(0, 2)
     shift_delta(2, 2)
-    sum1.along_y()
+    sum1.plane()
     input_delta(0, 0)
-    sum2.along_x()
     input_delta(0, 1)
     sum1.along_z()
     sum2.gather_z()
@@ -450,8 +455,7 @@
     d1e[4, 0, 0:16] = jnp.where(top, jnp.zeros((16, 16, 128), BF), d1e[4, 0, 0:16])
     shift_delta(4, 1)
     input_delta(1, 0)
-    sum1.along_x()
-    sum2.gather_y()
+    sum2.gather_plane()
     input_delta(1, 1)
     sum1.gather_z()
 
@@ -460,20 +464,17 @@
         lanes = pl.ds(pl.multiple_of(c * 256, 256), 256)
         ig[:, lanes] = dot(p4[...], un[:, :, lanes].reshape(256, 256)).astype(BF)
 
-    sum1.gather_y()
+    sum1.gather_plane()
     sum2.finish()
     whole = bufs2[-1]
-    for block in range(54):
-        flat = block * 32
-        k = flat // piece2
-        got = whole[k // NZ, k % NZ, flat % piece2 : flat % piece2 + 32].astype(F32) * scales[1]
-        g2out[flat % 864 : flat % 864 + 32, flat // 864 * 128 : (flat // 864 + 1) * 128] = got
+    for row, count, g, k, at_row in pieces(0, 1728, GROUP2, PIECE2):
+        got = whole[g // 2, g % 2, k, at_row : at_row + count].astype(F32) * scales[1]
+        half = row // 864
+        g2out[row % 864 : row % 864 + count, half * 128 : (half + 1) * 128] = got
     sum1.finish()
     whole = bufs1[-1]
-    for block in range(27):
-        flat = block * 16
-        k = flat // piece1
-        g1out[flat : flat + 16] = whole[k // NZ, k % NZ, flat % piece1 : flat % piece1 + 16].astype(F32) * scales[0]
+    for row, count, g, k, at_row in pieces(0, 432, GROUP1, PIECE1):
+        g1out[row : row + count] = whole[g // 2, g % 2, k].astype(F32) * scales[0]
 
     for copy in sent + passed + [halo_in, halo_hid, halo_d2, halo_d1]:
         copy.wait_send()
@@ -518,8 +519,8 @@
             pltpu.SemaphoreType.DMA((2, 10)),
             pltpu.SemaphoreType.DMA((2, 4)),
         ]
-        + Reduction.scratch(R1ROWS)
-        + Reduction.scratch(R2ROWS),
+        + Reduction.scratch(PIECE1)
+        + Reduction.scratch(PIECE2),
         compiler_params=pltpu.CompilerParams(
             collective_id=0, has_side_effects=True, vmem_limit_bytes=60 * 1024 * 1024
         ),

time: 76.6 us -> 74.8 us (0.977)
  Pallas kernels: 70.2 us -> 68.5 us
    pallas_call x1, Pallas kernels: 70.2 us -> 68.5 us  [local(): pl.pallas_call(body, out_shape=(shape((2, 8, 2048), BF), shape((256, 2048...]
where the time goes in v2:
time: 74.8 us; the launch traced here: 74.6 us
  Pallas kernels  68.5 us (92%)
  local copies, waits for them, and re-layouts  5.47 us (7%)
    pallas_call x1, Pallas kernels, local(): pl.pallas_call(body, out_shape=(shape((2, 8, 2048), BF), shape((256, 2048...  68.5 us
    unnamed x8, local copies, waits for them, and re-layouts  5.47 us

profile of v2, /device:TPU:8, one launch (start us, length us, event | category | flops | bytes accessed | tf_op | source)
XLA Modules:
  0.0 74.6 jit_solution(10131757237354751774)
XLA Ops:
  0.6 68.5 %step.1 = (bf16[2,8,2048]{2,1,0:T(8,128)(2,1)}, bf16[256,2048]{1,0:T(8,128)(2,1)}, f32[432,128]{1,0:T(8,128)}, f32[864,256]{1,0:T(8,128)}) custom-call(bf16[256,2048]{1,0:T(8,128)(2,1)} %bitcast.4, bf16[432,128]{1,0:T(8,128)(2,1)} %refs_1_.1, bf16[864,256]{1,0:T(8,128)(2,1)} %refs_2_.1, bf16[2,8,2048]{2,1,0:T(8,128)(2,1)} %bitcast.6, ...), custom_call_target="tpu_custom_call" | custom-call | tf_op jit(solution)/shard_map/step/pallas_call | solution.py:494
  69.2 1.5 %copy.17 = bf16[1,2,8,2048]{3,2,1,0:T(8,128)(2,1)} copy(bf16[1,2,8,2048]{3,2,1,0:T(8,128)(2,1)} %bitcast.7) | data formatting | bytes 131072
  70.6 0.0 copy-start.1
  70.6 0.0 copy-start
  70.6 2.4 %copy.18 = bf16[1,8,32,2048]{3,2,1,0:T(8,128)(2,1)} copy(bf16[1,8,32,2048]{3,2,1,0:T(8,128)(2,1)} %bitcast.5) | data formatting | bytes 2097152
  73.0 0.0 copy-done.1
  73.0 0.7 copy.19
  73.7 0.0 copy-done
  73.7 0.9 %copy.20 = f32[864,256]{1,0:T(8,128)} copy(f32[864,256]{1,0:T(8,128)S(1)} %copy-done) | data formatting | bytes 1769472
Async XLA Ops:
  70.6 2.4 %copy-start.1 = (f32[432,128]{1,0:T(8,128)S(1)}, f32[432,128]{1,0:T(8,128)}, u32[]{:S(2)}) copy-start(f32[432,128]{1,0:T(8,128)} %get-tuple-element.18) | copy-start | bytes 663556
  70.6 3.1 %copy-start = (f32[864,256]{1,0:T(8,128)S(1)}, f32[864,256]{1,0:T(8,128)}, u32[]{:S(2)}) copy-start(f32[864,256]{1,0:T(8,128)} %get-tuple-element.19) | copy-start | bytes 2654212

commit v3 on v2

--- a/solution.py
+++ b/solution.py
@@ -168,20 +168,21 @@
         for j in range(NZ - 1):
             total += self.r3[j].astype(F32)
         self.g[y, xh, z] = total.astype(BF)
-        self.fifth = []
+        self.fifth = {}
         for k in far_first(NZ):
-            self.fifth.append(self.send(self.g.at[y, xh, z], self.g.at[y, xh, z], self.peers["z", k]))
+            self.fifth[k] = self.send(self.g.at[y, xh, z], self.g.at[y, xh, z], self.peers["z", k])
 
     def gather_plane(self):
         xl, core, y, z, xh = self.at
-        for copy in self.fifth:
-            copy.wait_recv()
         self.sixth = []
-        part = self.g.at[y, xh, pl.ds(0, USED)]
-        for k in far_first(NY) + [0]:
-            for v in (1, 0):
-                if (k, v) != (0, 0):
-                    self.sixth.append(self.send(part, part, self.peers["plane", k, 0, v]))
+        for k in [0] + sorted(self.fifth, key=lambda k: min(k, NZ - k)):
+            if k:
+                self.fifth[k].wait_recv()
+            part = self.g.at[y, xh, (z + NZ - k) % NZ]
+            for j in far_first(NY) + [0]:
+                for v in (1, 0):
+                    if (j, v) != (0, 0):
+                        self.sixth.append(self.send(part, part, self.peers["plane", j, 0, v]))
 
     def finish(self):
         for copy in self.sixth:
@@ -202,7 +203,99 @@
             pltpu.VMEM((NZ, piece, 128), BF),
             pltpu.VMEM((NZ - 1, piece, 128), BF),
             pltpu.VMEM((NY, 2, NZ, piece, 128), BF),
-            pltpu.SemaphoreType.DMA((2, 2 * NY + (4 * NY - 1) + 2 * (NZ - 1) + (2 * NY - 1))),
+            pltpu.SemaphoreType.DMA((2, 2 * NY + (4 * NY - 1) + 2 * (NZ - 1) + NZ * (2 * NY - 1))),
+        ]
+
+
+class LineReduction(Reduction):
+    def cores(self):
+        xl, core, y, z, xh = self.at
+        self.first = []
+        for h in range(2):
+            self.first.append(
+                self.send(
+                    self.s.at[h * 2 + 1 - core, :, pl.ds(0, USED)], self.r1.at[h, :, pl.ds(0, USED)], self.peers["core"]
+                )
+            )
+
+    def along_z(self):
+        xl, core, y, z, xh = self.at
+        for copy in self.first:
+            copy.wait_recv()
+        self.second = []
+        for k in far_first(NZ) + [0]:
+            there = (z + k) % NZ
+            for h in range(2):
+                for i in range(USED):
+                    mine = self.s[h * 2 + core, there, i].astype(F32)
+                    self.hy[k, h, i] = (mine + self.r1[h, there, i].astype(F32)).astype(BF)
+            if k:
+                self.second.append(
+                    self.send(
+                        self.hy.at[k, :, pl.ds(0, USED)], self.r2.at[k - 1, :, pl.ds(0, USED)], self.peers["z", k]
+                    )
+                )
+
+    def plane(self):
+        xl, core, y, z, xh = self.at
+        for copy in self.second:
+            copy.wait_recv()
+        for h in range(2):
+            for i in range(USED):
+                total = self.hy[0, h, i].astype(F32)
+                for j in range(NZ - 1):
+                    total += self.r2[j, h, i].astype(F32)
+                self.hz[h, i] = total.astype(BF)
+            self.hz[h, USED:] = jnp.zeros_like(self.hz[h, USED:])
+        self.third = []
+        for k in far_first(NY) + [0]:
+            for h in range(2):
+                for v in range(2):
+                    if (k, h, v) != (0, 0, 0):
+                        left = xl + h - 2 * xl * h
+                        group = (y + k) % NY * 2 + xh + v - 2 * xh * v
+                        self.third.append(
+                            self.send(self.hz.at[left, group], self.r3.at[k, h, v], self.peers["plane", k, h, v])
+                        )
+
+    def gather_plane(self):
+        xl, core, y, z, xh = self.at
+        for copy in self.third:
+            copy.wait_recv()
+        mine = y * 2 + xh
+        total = self.hz[xl, mine].astype(F32)
+        for k in range(NY):
+            for h in range(2):
+                for v in range(2):
+                    if (k, h, v) != (0, 0, 0):
+                        total += self.r3[k, h, v].astype(F32)
+        self.g[z, mine] = total.astype(BF)
+        self.fifth = []
+        for k in far_first(NY) + [0]:
+            for v in (1, 0):
+                if (k, v) != (0, 0):
+                    self.fifth.append(self.send(self.g.at[z, mine], self.g.at[z, mine], self.peers["plane", k, 0, v]))
+
+    def gather_z(self):
+        xl, core, y, z, xh = self.at
+        for copy in self.fifth:
+            copy.wait_recv()
+        self.sixth = []
+        part = self.g.at[z, pl.ds(0, USED)]
+        for k in far_first(NZ):
+            self.sixth.append(self.send(part, part, self.peers["z", k]))
+
+    @staticmethod
+    def scratch(piece):
+        return [
+            pltpu.VMEM((4, NZ, 2 * NY, piece, 128), BF),
+            pltpu.VMEM((2, NZ, 2 * NY, piece, 128), BF),
+            pltpu.VMEM((NZ, 2, 2 * NY, piece, 128), BF),
+            pltpu.VMEM((NZ - 1, 2, 2 * NY, piece, 128), BF),
+            pltpu.VMEM((2, 2 * NY, piece, 128), BF),
+            pltpu.VMEM((NY, 2, 2, piece, 128), BF),
+            pltpu.VMEM((NZ, 2 * NY, piece, 128), BF),
+            pltpu.SemaphoreType.DMA((2, 2 + 2 * (NZ - 1) + (4 * NY - 1) + (2 * NY - 1))),
         ]
 
 
@@ -362,7 +455,7 @@
                     h = half * NY + g
                     s2[q, h // 2, h % 2, k, at_row : at_row + count] = block
     sum2 = Reduction(s2, bufs2, sems2, peers)
-    sum1 = Reduction(s1, bufs1, sems1, peers)
+    sum1 = LineReduction(s1, bufs1, sems1, peers)
     sum2.cores()
 
     def spread_delta(o):
@@ -419,10 +512,9 @@
         for k in range(24):
             block = t * 24 + k
             g = block % 54 // 7
-            s1[block // 54, g // 2, g % 2, block % 54 % 7] = got[64 + k * 8 : 64 + (k + 1) * 8].astype(BF)
+            s1[block // 54, g, block % 54 % 7] = got[64 + k * 8 : 64 + (k + 1) * 8].astype(BF)
 
     sum1.cores()
-    sum2.along_z()
 
     def shift_delta(first, count):
         both = jnp.concatenate([d1e[first + k, 0, 0:16].reshape(256, 128) for k in range(count)], axis=1)
@@ -446,25 +538,26 @@
 
     shift_delta(0, 2)
     shift_delta(2, 2)
-    sum1.plane()
     input_delta(0, 0)
+    sum1.along_z()
     input_delta(0, 1)
-    sum1.along_z()
-    sum2.gather_z()
     halo_d1.wait_recv()
     d1e[4, 0, 0:16] = jnp.where(top, jnp.zeros((16, 16, 128), BF), d1e[4, 0, 0:16])
     shift_delta(4, 1)
     input_delta(1, 0)
-    sum2.gather_plane()
     input_delta(1, 1)
-    sum1.gather_z()
 
     @pl.loop(0, 8)
     def _(c):
         lanes = pl.ds(pl.multiple_of(c * 256, 256), 256)
         ig[:, lanes] = dot(p4[...], un[:, :, lanes].reshape(256, 256)).astype(BF)
 
+    sum2.along_z()
+    sum1.plane()
+    sum2.gather_z()
     sum1.gather_plane()
+    sum2.gather_plane()
+    sum1.gather_z()
     sum2.finish()
     whole = bufs2[-1]
     for row, count, g, k, at_row in pieces(0, 1728, GROUP2, PIECE2):
@@ -474,7 +567,7 @@
     sum1.finish()
     whole = bufs1[-1]
     for row, count, g, k, at_row in pieces(0, 432, GROUP1, PIECE1):
-        g1out[row : row + count] = whole[g // 2, g % 2, k].astype(F32) * scales[0]
+        g1out[row : row + count] = whole[g, k].astype(F32) * scales[0]
 
     for copy in sent + passed + [halo_in, halo_hid, halo_d2, halo_d1]:
         copy.wait_send()
@@ -519,7 +612,7 @@
             pltpu.SemaphoreType.DMA((2, 10)),
             pltpu.SemaphoreType.DMA((2, 4)),
         ]
-        + Reduction.scratch(PIECE1)
+        + LineReduction.scratch(PIECE1)
         + Reduction.scratch(PIECE2),
         compiler_params=pltpu.CompilerParams(
             collective_id=0, has_side_effects=True, vmem_limit_bytes=60 * 1024 * 1024

time: 74.8 us -> 68.6 us (0.917); the launches traced: 74.6 us -> 67.5 us
  Pallas kernels: 68.5 us -> 61.4 us
    pallas_call x1, Pallas kernels: 68.5 us -> 61.4 us  [local(): pl.pallas_call(body, out_shape=(shape((2, 8, 2048), BF), shape((256, 2048...]
where the time goes in v3:
time: 68.6 us; the launch traced here: 67.5 us
  Pallas kernels  61.4 us (90%)
  local copies, waits for them, and re-layouts  5.47 us (8%)
    pallas_call x1, Pallas kernels, local(): pl.pallas_call(body, out_shape=(shape((2, 8, 2048), BF), shape((256, 2048...  61.4 us
    unnamed x8, local copies, waits for them, and re-layouts  5.47 us

profile of v3, /device:TPU:8, one launch (start us, length us, event | category | flops | bytes accessed | tf_op | source)
XLA Modules:
  0.0 67.5 jit_solution(3957548958855940220)
XLA Ops:
  0.6 61.4 %step.1 = (bf16[2,8,2048]{2,1,0:T(8,128)(2,1)}, bf16[256,2048]{1,0:T(8,128)(2,1)}, f32[432,128]{1,0:T(8,128)}, f32[864,256]{1,0:T(8,128)}) custom-call(bf16[256,2048]{1,0:T(8,128)(2,1)} %bitcast.4, bf16[432,128]{1,0:T(8,128)(2,1)} %refs_1_.1, bf16[864,256]{1,0:T(8,128)(2,1)} %refs_2_.1, bf16[2,8,2048]{2,1,0:T(8,128)(2,1)} %bitcast.6, ...), custom_call_target="tpu_custom_call" | custom-call | tf_op jit(solution)/shard_map/step/pallas_call | solution.py:587
  62.1 1.5 %copy.17 = bf16[1,2,8,2048]{3,2,1,0:T(8,128)(2,1)} copy(bf16[1,2,8,2048]{3,2,1,0:T(8,128)(2,1)} %bitcast.7) | data formatting | bytes 131072
  63.5 0.0 copy-start.1
  63.5 0.0 copy-start
  63.5 2.4 %copy.18 = bf16[1,8,32,2048]{3,2,1,0:T(8,128)(2,1)} copy(bf16[1,8,32,2048]{3,2,1,0:T(8,128)(2,1)} %bitcast.5) | data formatting | bytes 2097152
  65.9 0.0 copy-done.1
  65.9 0.7 %copy.19 = f32[432,128]{1,0:T(8,128)} copy(f32[432,128]{1,0:T(8,128)S(1)} %copy-done.1) | data formatting | bytes 442368
  66.6 0.0 copy-done
  66.6 0.9 %copy.20 = f32[864,256]{1,0:T(8,128)} copy(f32[864,256]{1,0:T(8,128)S(1)} %copy-done) | data formatting | bytes 1769472
Async XLA Ops:
  63.5 2.4 %copy-start.1 = (f32[432,128]{1,0:T(8,128)S(1)}, f32[432,128]{1,0:T(8,128)}, u32[]{:S(2)}) copy-start(f32[432,128]{1,0:T(8,128)} %get-tuple-element.18) | copy-start | bytes 663556
  63.5 3.1 %copy-start = (f32[864,256]{1,0:T(8,128)S(1)}, f32[864,256]{1,0:T(8,128)}, u32[]{:S(2)}) copy-start(f32[864,256]{1,0:T(8,128)} %get-tuple-element.19) | copy-start | bytes 2654212

commit v4 on v3

--- a/solution.py
+++ b/solution.py
@@ -11,6 +11,8 @@
 BF, F32 = jnp.bfloat16, jnp.float32
 PIECE1, PIECE2 = 8, 32
 GROUP1, GROUP2 = 56, 216
+VLIM = 40
+OUT = pltpu.VMEM
 USED = 7
 MESH = pl.DeviceIdType.MESH
 
@@ -202,7 +204,6 @@
             pltpu.VMEM(blocks, BF),
             pltpu.VMEM((NZ, piece, 128), BF),
             pltpu.VMEM((NZ - 1, piece, 128), BF),
-            pltpu.VMEM((NY, 2, NZ, piece, 128), BF),
             pltpu.SemaphoreType.DMA((2, 2 * NY + (4 * NY - 1) + 2 * (NZ - 1) + NZ * (2 * NY - 1))),
         ]
 
@@ -294,16 +295,46 @@
             pltpu.VMEM((NZ - 1, 2, 2 * NY, piece, 128), BF),
             pltpu.VMEM((2, 2 * NY, piece, 128), BF),
             pltpu.VMEM((NY, 2, 2, piece, 128), BF),
-            pltpu.VMEM((NZ, 2 * NY, piece, 128), BF),
             pltpu.SemaphoreType.DMA((2, 2 + 2 * (NZ - 1) + (4 * NY - 1) + (2 * NY - 1))),
         ]
 
 
-def step_kernel(scales, vol, w1, w2, cot, p0, p1, p2, p3, p4, actv, ig, g1out, g2out, *scratch):
+def pieces(lo, hi, group, piece):
+    while lo < hi:
+        where = lo % group
+        count = min(hi - lo, group - where, piece - where % piece)
+        yield lo, count, lo // group, where // piece, where % piece
+        lo += count
+
+
+def finish_kernel(scales, actv, ig, g1, g2, actv_out, ig_out, g1out, g2out, sems):
+    copies = [pltpu.make_async_copy(ig, ig_out, sems.at[0]), pltpu.make_async_copy(actv, actv_out, sems.at[1])]
+    for copy in copies:
+        copy.start()
+    for row, count, g, k, at_row in pieces(0, 1728, GROUP2, PIECE2):
+        got = g2[g // 2, g % 2, k, at_row : at_row + count].astype(F32) * scales[1]
+        half = row // 864
+        g2out[row % 864 : row % 864 + count, half * 128 : (half + 1) * 128] = got
+    for row, count, g, k, at_row in pieces(0, 432, GROUP1, PIECE1):
+        g1out[row : row + count] = g1[g, k].astype(F32) * scales[0]
+    for copy in copies:
+        copy.wait()
+
+
+def step_kernel(vol_in, w1, w2, cot_in, p0_in, p1_in, p2_in, p3_in, p4_in, actv, ig, g1, g2, *scratch):
+    vol, cot, p0, p1, p2, p3, p4, lsem = scratch[30:]
+    loads = []
+    for k, (src, dst) in enumerate(
+        ((vol_in, vol), (p0_in, p0), (p1_in, p1), (cot_in, cot), (p2_in, p2), (p3_in, p3), (p4_in, p4))
+    ):
+        loads.append(pltpu.make_async_copy(src, dst, lsem.at[k]))
+        loads[-1].start()
     xe, xhalo, w1g, w1p, wb, w2g, hid, hhalo, slope, l2, d2, d2e, d1e, un = scratch[:14]
     wsem, hsem = scratch[14:16]
-    s1, *bufs1, sems1 = scratch[16:24]
-    s2, *bufs2, sems2 = scratch[24:32]
+    s1, *bufs1, sems1 = scratch[16:23]
+    s2, *bufs2, sems2 = scratch[23:30]
+    bufs1.append(g1)
+    bufs2.append(g2)
     at = xl, core, y, z, xh = place()
     s, d = lax.axis_index("space"), lax.axis_index("dp")
     n = 2 * NY * NZ
@@ -321,6 +352,12 @@
         peers["z", k] = device(xl, core, y, (z + k) % NZ, xh)
     peers["upper"], peers["lower"] = upper, lower
 
+    held = []
+    for k, (src, dst, size) in enumerate(((w1, w1g, 432), (w2, w2g, 864))):
+        at_rows = pl.ds(pl.multiple_of(d * size, 16), size)
+        held.append(pltpu.make_async_copy(src, dst.at[at_rows], lsem.at[7 + k]))
+        held[-1].start()
+
     barrier = pltpu.get_barrier_semaphore()
     for peer in peers.values():
         pl.semaphore_signal(barrier, inc=1, device_id=peer, device_id_type=MESH)
@@ -342,7 +379,7 @@
         forward.append((whole, size, parts, arriving, to_core, base))
         sent += arriving + [to_core]
         if slot == 0:
-            halo_in = remote(vol.at[pl.ds(224, 32)], xhalo, hsem, 0, upper)
+            halo_in = remote(vol_in.at[pl.ds(224, 32)], xhalo, hsem, 0, upper)
 
     passed = []
 
@@ -355,6 +392,8 @@
         return to_core, passed[-2:]
 
     xe[:, :, 0] = jnp.zeros((9, 3, 16, 128), BF)
+    for copy in loads + held:
+        copy.wait()
 
     @pl.loop(0, 8)
     def _(c):
@@ -364,8 +403,6 @@
                 for u in range(2):
                     xe[i + 1, e, 2 * c + 1 + u] = got[(i * 3 + e) * 16 : (i * 3 + e + 1) * 16, u * 128 : (u + 1) * 128]
 
-    w1g[rows(d, 432, 0, 432)] = w1[...]
-    w2g[rows(d, 864, 0, 864)] = w2[...]
     to_core, others = pass_on(0)
     to_core.wait_recv()
     for copy in others:
@@ -436,13 +473,6 @@
         for q in range(8):
             at_row = (o * 8 + q) * 8
             actv[o, :, q * 256 : (q + 1) * 256] = value[at_row : at_row + 8].astype(BF)
-
-    def pieces(lo, hi, group, piece):
-        while lo < hi:
-            where = lo % group
-            count = min(hi - lo, group - where, piece - where % piece)
-            yield lo, count, lo // group, where // piece, where % piece
-            lo += count
 
     for t in range(27):
         got = dot(l2[:, t * 128 : (t + 1) * 128], delta, 0, 0)
@@ -559,16 +589,7 @@
     sum2.gather_plane()
     sum1.gather_z()
     sum2.finish()
-    whole = bufs2[-1]
-    for row, count, g, k, at_row in pieces(0, 1728, GROUP2, PIECE2):
-        got = whole[g // 2, g % 2, k, at_row : at_row + count].astype(F32) * scales[1]
-        half = row // 864
-        g2out[row % 864 : row % 864 + count, half * 128 : (half + 1) * 128] = got
     sum1.finish()
-    whole = bufs1[-1]
-    for row, count, g, k, at_row in pieces(0, 432, GROUP1, PIECE1):
-        g1out[row : row + count] = whole[g, k].astype(F32) * scales[0]
-
     for copy in sent + passed + [halo_in, halo_hid, halo_d2, halo_d1]:
         copy.wait_send()
     sum2.drain()
@@ -579,20 +600,19 @@
     cells = 4 * lax.axis_size("space") * 4 * 256
     scales = (float(cells) ** -0.5, float(cells // 8) ** -0.5)
     vmem = pl.BlockSpec(memory_space=pltpu.VMEM)
+    anywhere = pl.BlockSpec(memory_space=pl.ANY)
+    far = pl.BlockSpec(memory_space=pltpu.HBM)
     shape = jax.ShapeDtypeStruct
 
-    def body(*refs):
-        step_kernel(scales, *refs)
-
-    activations, input_gradient, first, second = pl.pallas_call(
-        body,
+    partial = pl.pallas_call(
+        step_kernel,
         out_shape=(
-            shape((2, 8, 2048), BF),
-            shape((256, 2048), BF),
-            shape((432, 128), F32),
-            shape((864, 256), F32),
+            OUT((2, 8, 2048), BF),
+            OUT((256, 2048), BF),
+            OUT((NZ, 2 * NY, PIECE1, 128), BF),
+            OUT((NY, 2, NZ, PIECE2, 128), BF),
         ),
-        in_specs=[vmem] * 9,
+        in_specs=[far] * 9,
         out_specs=(vmem,) * 4,
         scratch_shapes=[
             pltpu.VMEM((9, 3, 17, 16, 128), BF),
@@ -613,18 +633,51 @@
             pltpu.SemaphoreType.DMA((2, 4)),
         ]
         + LineReduction.scratch(PIECE1)
-        + Reduction.scratch(PIECE2),
+        + Reduction.scratch(PIECE2)
+        + [
+            pltpu.VMEM((256, 2048), BF),
+            pltpu.VMEM((2, 8, 2048), BF),
+            pltpu.VMEM((384, 256), BF),
+            pltpu.VMEM((576, 256), BF),
+            pltpu.VMEM((256, 64), BF),
+            pltpu.VMEM((256, 256), BF),
+            pltpu.VMEM((256, 256), BF),
+            pltpu.SemaphoreType.DMA((9,)),
+        ],
         compiler_params=pltpu.CompilerParams(
-            collective_id=0, has_side_effects=True, vmem_limit_bytes=60 * 1024 * 1024
+            collective_id=0, has_side_effects=True, vmem_limit_bytes=VLIM * 1024 * 1024
         ),
         name="step",
     )(
-        volume.reshape(256, 2048),
-        weight_first,
-        weight_second,
-        cotangent.reshape(2, 8, 2048),
-        *selections(),
+        *(
+            pltpu.with_memory_space_constraint(x, pltpu.HBM)
+            for x in (
+                volume.reshape(256, 2048),
+                weight_first,
+                weight_second,
+                cotangent.reshape(2, 8, 2048),
+                *(jnp.asarray(m) for m in selections()),
+            )
+        )
     )
+
+    def body(*refs):
+        finish_kernel(scales, *refs)
+
+    activations, input_gradient, first, second = pl.pallas_call(
+        body,
+        out_shape=(
+            shape((2, 8, 2048), BF),
+            shape((256, 2048), BF),
+            shape((432, 128), F32),
+            shape((864, 256), F32),
+        ),
+        in_specs=[vmem] * 4,
+        out_specs=(anywhere, anywhere, vmem, vmem),
+        scratch_shapes=[pltpu.SemaphoreType.DMA((2,))],
+        compiler_params=pltpu.CompilerParams(vmem_limit_bytes=8 * 1024 * 1024),
+        name="finish",
+    )(*(pltpu.with_memory_space_constraint(x, pltpu.VMEM) for x in partial))
     return (
         activations.reshape(cotangent.shape),
         input_gradient.reshape(volume.shape),

time: 68.6 us -> 62.4 us (0.910)
  local copies, waits for them, and re-layouts: 5.47 us -> 0 us
    pallas_call x1, Pallas kernels: 61.4 us -> 1.98 us  [local(): pl.pallas_call(body, out_shape=(shape((2, 8, 2048), BF), shape((256, 2048...]
    pallas_call x0 -> x1, Pallas kernels: none -> 58.8 us  [local(): pl.pallas_call(step_kernel, out_shape=(OUT((2, 8, 2048), BF), OUT((256, 2...]
    unnamed x8 -> x0, local copies, waits for them, and re-layouts: 5.47 us -> none
where the time goes in v4:
time: 62.4 us; the launch traced here: 61.5 us
  Pallas kernels  60.8 us (97%)
  between operations  0.64 us (1%)
    pallas_call x1, Pallas kernels, local(): pl.pallas_call(step_kernel, out_shape=(OUT((2, 8, 2048), BF), OUT((256, 2...  58.8 us
    pallas_call x1, Pallas kernels, local(): pl.pallas_call(body, out_shape=(shape((2, 8, 2048), BF), shape((256, 2048...  1.98 us

profile of v4, /device:TPU:8, one launch (start us, length us, event | category | flops | bytes accessed | tf_op | source)
XLA Modules:
  0.0 61.5 jit_solution(15225557128044139352)
XLA Ops:
  0.6 58.8 %step.1 = (bf16[2,8,2048]{2,1,0:T(8,128)(2,1)S(1)}, bf16[256,2048]{1,0:T(8,128)(2,1)S(1)}, bf16[8,8,8,128]{3,2,1,0:T(8,128)(2,1)S(1)}, bf16[4,2,8,32,128]{4,3,2,1,0:T(8,128)(2,1)S(1)}) custom-call(bf16[256,2048]{1,0:T(8,128)(2,1)} %bitcast.4, bf16[432,128]{1,0:T(8,128)(2,1)} %w1.1, bf16[864,256]{1,0:T(8,128)(2,1)} %w2.1, bf16[2,8,2048]{2,1,0:T(8,128)(2,1)} %bitcast.5, ...), custom_call_target="tpu_custom_call" | custom-call | tf_op jit(solution)/shard_map/step/pallas_call | solution.py:607
  59.5 2.0 %finish.1 = (bf16[2,8,2048]{2,1,0:T(8,128)(2,1)}, bf16[256,2048]{1,0:T(8,128)(2,1)}, f32[432,128]{1,0:T(8,128)}, f32[864,256]{1,0:T(8,128)}) custom-call(bf16[2,8,2048]{2,1,0:T(8,128)(2,1)S(1)} %get-tuple-element.12.refs_0_, bf16[256,2048]{1,0:T(8,128)(2,1)S(1)} %get-tuple-element.13.refs_1_, bf16[8,8,8,128]{3,2,1,0:T(8,128)(2,1)S(1)} %get-tuple-element.14.refs_2_, ...), custom_call_target="tpu_custom_call" | custom-call | tf_op jit(solution)/shard_map/finish/pallas_call | solution.py:667

commit v5 on v4

--- a/solution.py
+++ b/solution.py
@@ -95,13 +95,21 @@
     return sorted(range(1, n), key=lambda k: -min(k, n - k))
 
 
+COLUMNS = [(0, 1), (1, 0), (1, 1)]
+CUT = 3
+
+
 class Reduction:
     def __init__(self, s, bufs, sems, peers):
         self.s, self.sems, self.peers = s, sems, peers
-        self.r1, self.hy, self.r2, self.hz, self.r3, self.g = bufs
+        self.name(*bufs)
         self.copies = []
         self.slot = 0
         self.at = place()
+
+    def name(self, r1, hy, r2, tx, r3x, ty, r3y, tot, r3, g):
+        self.r1, self.hy, self.r2, self.tx, self.r3x, self.ty, self.r3y, self.tot = r1, hy, r2, tx, r3x, ty, r3y, tot
+        self.r3, self.g = r3, g
 
     def send(self, src, dst, target):
         copy = remote(src, dst, self.sems, self.slot, target)
@@ -124,7 +132,7 @@
 
     def plane(self):
         xl, core, y, z, xh = self.at
-        self.second = []
+        self.lines_x, self.lines_y = {}, {}
         for k in self.order:
             there = (y + k) % NY
             for h in range(2):
@@ -136,37 +144,60 @@
                     for i in range(USED):
                         mine = self.s[left * 2 + core, there, half, i].astype(F32)
                         self.hy[k, h, v, i] = (mine + self.r1[k, left, half, i].astype(F32)).astype(BF)
-                    if (k, h, v) != (0, 0, 0):
-                        self.second.append(
-                            self.send(
-                                self.hy.at[k, h, v, pl.ds(0, USED)],
-                                self.r2.at[k, h, v, pl.ds(0, USED)],
-                                self.peers["plane", k, h, v],
-                            )
-                        )
+            if k:
+                part = (k, slice(None), slice(None), pl.ds(CUT, USED - CUT))
+                self.lines_y[k] = self.send(self.hy.at[part], self.r2.at[part], self.peers["plane", k, 0, 0])
+        for h, v in COLUMNS:
+            part = (slice(None), h, v, pl.ds(0, CUT))
+            self.lines_x[h, v] = self.send(self.hy.at[part], self.r2.at[part], self.peers["plane", 0, h, v])
+
+    def turn(self):
+        self.second = []
+        for copy in self.lines_x.values():
+            copy.wait_recv()
+        for k in self.order:
+            for i in range(CUT):
+                total = self.hy[k, 0, 0, i].astype(F32)
+                for h, v in COLUMNS:
+                    total += self.r2[k, h, v, i].astype(F32)
+                self.tx[k, i] = total.astype(BF)
+            if k:
+                self.second.append(self.send(self.tx.at[k], self.r3x.at[k], self.peers["plane", k, 0, 0]))
+        for copy in self.lines_y.values():
+            copy.wait_recv()
+        for h, v in COLUMNS + [(0, 0)]:
+            for i in range(CUT, USED):
+                total = self.hy[0, h, v, i].astype(F32)
+                for k in range(1, NY):
+                    total += self.r2[k, h, v, i].astype(F32)
+                self.ty[h, v, i - CUT] = total.astype(BF)
+            if h or v:
+                self.second.append(self.send(self.ty.at[h, v], self.r3y.at[h, v], self.peers["plane", 0, h, v]))
 
     def along_z(self):
         xl, core, y, z, xh = self.at
         for copy in self.second:
             copy.wait_recv()
+        for i in range(CUT):
+            total = self.tx[0, i].astype(F32)
+            for k in range(1, NY):
+                total += self.r3x[k, i].astype(F32)
+            self.tot[i] = total.astype(BF)
+        for i in range(USED - CUT):
+            total = self.ty[0, 0, i].astype(F32)
+            for h, v in COLUMNS:
+                total += self.r3y[h, v, i].astype(F32)
+            self.tot[CUT + i] = total.astype(BF)
+        self.tot[USED:] = jnp.zeros_like(self.tot[USED:])
         self.third = []
-        for k in far_first(NZ) + [0]:
-            there = (z + k) % NZ
-            total = self.hy[0, 0, 0, there].astype(F32)
-            for j in range(NY):
-                for h in range(2):
-                    for v in range(2):
-                        if (j, h, v) != (0, 0, 0):
-                            total += self.r2[j, h, v, there].astype(F32)
-            self.hz[k] = total.astype(BF)
-            if k:
-                self.third.append(self.send(self.hz.at[k], self.r3.at[k - 1], self.peers["z", k]))
+        for k in far_first(NZ):
+            self.third.append(self.send(self.tot.at[(z + k) % NZ], self.r3.at[k - 1], self.peers["z", k]))
 
     def gather_z(self):
         xl, core, y, z, xh = self.at
         for copy in self.third:
             copy.wait_recv()
-        total = self.hz[0].astype(F32)
+        total = self.tot[z].astype(F32)
         for j in range(NZ - 1):
             total += self.r3[j].astype(F32)
         self.g[y, xh, z] = total.astype(BF)
@@ -202,13 +233,20 @@
             pltpu.VMEM(blocks, BF),
             pltpu.VMEM(blocks, BF),
             pltpu.VMEM(blocks, BF),
+            pltpu.VMEM((NY, CUT, piece, 128), BF),
+            pltpu.VMEM((NY, CUT, piece, 128), BF),
+            pltpu.VMEM((2, 2, USED - CUT, piece, 128), BF),
+            pltpu.VMEM((2, 2, USED - CUT, piece, 128), BF),
             pltpu.VMEM((NZ, piece, 128), BF),
             pltpu.VMEM((NZ - 1, piece, 128), BF),
-            pltpu.SemaphoreType.DMA((2, 2 * NY + (4 * NY - 1) + 2 * (NZ - 1) + NZ * (2 * NY - 1))),
+            pltpu.SemaphoreType.DMA((2, 2 * NY + 2 * (NY + 2) + 2 * (NZ - 1) + NZ * (2 * NY - 1))),
         ]
 
 
 class LineReduction(Reduction):
+    def name(self, r1, hy, r2, hz, r3, g):
+        self.r1, self.hy, self.r2, self.hz, self.r3, self.g = r1, hy, r2, hz, r3, g
+
     def cores(self):
         xl, core, y, z, xh = self.at
         self.first = []
@@ -271,20 +309,21 @@
                     if (k, h, v) != (0, 0, 0):
                         total += self.r3[k, h, v].astype(F32)
         self.g[z, mine] = total.astype(BF)
-        self.fifth = []
+        self.fifth = {}
         for k in far_first(NY) + [0]:
             for v in (1, 0):
                 if (k, v) != (0, 0):
-                    self.fifth.append(self.send(self.g.at[z, mine], self.g.at[z, mine], self.peers["plane", k, 0, v]))
+                    self.fifth[k, v] = self.send(self.g.at[z, mine], self.g.at[z, mine], self.peers["plane", k, 0, v])
 
     def gather_z(self):
         xl, core, y, z, xh = self.at
-        for copy in self.fifth:
-            copy.wait_recv()
         self.sixth = []
-        part = self.g.at[z, pl.ds(0, USED)]
-        for k in far_first(NZ):
-            self.sixth.append(self.send(part, part, self.peers["z", k]))
+        for k, v in [(0, 0)] + sorted(self.fifth, key=lambda kv: min(kv[0], NY - kv[0]) + 2 * kv[1]):
+            if (k, v) != (0, 0):
+                self.fifth[k, v].wait_recv()
+            part = self.g.at[z, (y + NY - k) % NY * 2 + xh + v - 2 * xh * v]
+            for j in far_first(NZ):
+                self.sixth.append(self.send(part, part, self.peers["z", j]))
 
     @staticmethod
     def scratch(piece):
@@ -295,7 +334,7 @@
             pltpu.VMEM((NZ - 1, 2, 2 * NY, piece, 128), BF),
             pltpu.VMEM((2, 2 * NY, piece, 128), BF),
             pltpu.VMEM((NY, 2, 2, piece, 128), BF),
-            pltpu.SemaphoreType.DMA((2, 2 + 2 * (NZ - 1) + (4 * NY - 1) + (2 * NY - 1))),
+            pltpu.SemaphoreType.DMA((2, 2 + (NZ - 1) + (4 * NY - 1) + (2 * NY - 1) + 2 * NY * (NZ - 1))),
         ]
 
 
@@ -322,17 +361,17 @@
 
 
 def step_kernel(vol_in, w1, w2, cot_in, p0_in, p1_in, p2_in, p3_in, p4_in, actv, ig, g1, g2, *scratch):
-    vol, cot, p0, p1, p2, p3, p4, lsem = scratch[30:]
+    vol, cot, p0, p1, p2, p3, p4, lsem = scratch[35:]
     loads = []
     for k, (src, dst) in enumerate(
         ((vol_in, vol), (p0_in, p0), (p1_in, p1), (cot_in, cot), (p2_in, p2), (p3_in, p3), (p4_in, p4))
     ):
         loads.append(pltpu.make_async_copy(src, dst, lsem.at[k]))
         loads[-1].start()
-    xe, xhalo, w1g, w1p, wb, w2g, hid, hhalo, slope, l2, d2, d2e, d1e, un = scratch[:14]
-    wsem, hsem = scratch[14:16]
-    s1, *bufs1, sems1 = scratch[16:23]
-    s2, *bufs2, sems2 = scratch[23:30]
+    xe, xhalo, partial, w1g, w1p, wb, w2g, hid, hhalo, slope, l2, d2, d2e, d1e, un = scratch[:15]
+    wsem, hsem = scratch[15:17]
+    s1, *bufs1, sems1 = scratch[17:24]
+    s2, *bufs2, sems2 = scratch[24:35]
     bufs1.append(g1)
     bufs2.append(g2)
     at = xl, core, y, z, xh = place()
@@ -366,30 +405,31 @@
     def rows(q, size, lo, hi):
         return pl.ds(pl.multiple_of(q * size + lo, 16), hi - lo)
 
-    sent = []
-    forward = []
+    def weight(source, whole, size, cuts, base):
+        chunks, slot = [], base
+        middle = len(cuts) // 2
+        for k in range(middle):
+            chunk = []
+            for j, peer in ((k, peers["plane", 0, 1, 0]), (middle + k, peers["plane", 0, 1, 1])):
+                lo, hi = cuts[j], cuts[j + 1]
+                part = source.at[pl.ds(lo, hi - lo)]
+                chunk.append((lo, hi, remote(part, whole.at[rows(d, size, lo, hi)], wsem, slot, peer), slot + 1))
+                slot += 2
+            chunks.append(chunk)
+        to_core = remote(source, whole.at[rows(d, size, 0, size)], wsem, slot, peers["core"])
+        sent.extend([c[2] for chunk in chunks for c in chunk] + [to_core])
+        return chunks, to_core
+
+    sent, passed = [], []
     theirs = (1 - xl) * 2 + core
-    for slot, (own, whole, size, cut) in enumerate(((w1, w1g, 432, 224), (w2, w2g, 864, 432))):
-        base = slot * 5
-        parts = ((0, cut, peers["plane", 0, 1, 0]), (cut, size, peers["plane", 0, 1, 1]))
-        arriving = []
-        for j, (lo, hi, peer) in enumerate(parts):
-            arriving.append(remote(own.at[pl.ds(lo, hi - lo)], whole.at[rows(d, size, lo, hi)], wsem, base + j, peer))
-        to_core = remote(own, whole.at[rows(d, size, 0, size)], wsem, base + 2, peers["core"])
-        forward.append((whole, size, parts, arriving, to_core, base))
-        sent += arriving + [to_core]
-        if slot == 0:
-            halo_in = remote(vol_in.at[pl.ds(224, 32)], xhalo, hsem, 0, upper)
-
-    passed = []
-
-    def pass_on(slot):
-        whole, size, parts, arriving, to_core, base = forward[slot]
-        for j, (lo, hi, _) in enumerate(parts):
-            arriving[j].wait_recv()
+    chunks1, to_core1 = weight(w1, w1g, 432, (0, 224, 432), 0)
+    chunks2, to_core2 = weight(w2, w2g, 864, (0, 224, 432, 656, 864), 5)
+
+    def pass_on(whole, size, chunk):
+        for lo, hi, copy, slot in chunk:
+            copy.wait_recv()
             part = whole.at[rows(theirs, size, lo, hi)]
-            passed.append(remote(part, part, wsem, base + 3 + j, peers["core"]))
-        return to_core, passed[-2:]
+            passed.append(remote(part, part, wsem, slot, peers["core"]))
 
     xe[:, :, 0] = jnp.zeros((9, 3, 16, 128), BF)
     for copy in loads + held:
@@ -403,39 +443,40 @@
                 for u in range(2):
                     xe[i + 1, e, 2 * c + 1 + u] = got[(i * 3 + e) * 16 : (i * 3 + e + 1) * 16, u * 128 : (u + 1) * 128]
 
-    to_core, others = pass_on(0)
-    to_core.wait_recv()
-    for copy in others:
+    pass_on(w1g, 432, chunks1[0])
+    for copy in [to_core1] + passed:
         copy.wait_recv()
     for t in range(9):
         w1p[t * 256 : t * 256 + 64] = jnp.zeros((64, 128), BF)
         w1p[t * 256 + 64 : t * 256 + 256] = w1g[t * 192 : (t + 1) * 192]
 
-    def conv_first(o):
+    def pairs(plane, taps):
         tiles = []
-        for a in range(3):
+        for a in taps:
             for e in range(3):
-                tiles.append(xe[2 * o + a, e, 0:16].reshape(256, 128))
-                tiles.append(xe[2 * o + a, e, 1:17].reshape(256, 128))
-        value, gate = act_and_slope(dot(jnp.concatenate(tiles, axis=1), w1p[...]))
+                tiles.append(xe[plane + a, e, 0:16].reshape(256, 128))
+                tiles.append(xe[plane + a, e, 1:17].reshape(256, 128))
+        return jnp.concatenate(tiles, axis=1)
+
+    def finish_first(o, linear):
+        value, gate = act_and_slope(linear)
         hid[o] = value.astype(BF)
         slope[o] = gate.reshape(16, 16, 128)
 
-    conv_first(3)
+    partial[...] = dot(pairs(8, (0,)), w1p[0:768]).astype(BF)
+    halo_in = remote(partial, xhalo, hsem, 0, upper)
+    finish_first(3, dot(pairs(6, range(3)), w1p[...]))
     halo_hid = remote(hid.at[3], hhalo, hsem, 1, upper)
-    to_core_second, others_second = pass_on(1)
+    pass_on(w2g, 864, chunks2[0])
 
     @pl.loop(1, 3)
     def _(o):
-        conv_first(o)
-
+        finish_first(o, dot(pairs(2 * o, range(3)), w1p[...]))
+
+    pass_on(w2g, 864, chunks2[1])
+    local_first = dot(pairs(0, (1, 2)), w1p[768:])
     halo_in.wait_recv()
-    rim = jnp.where(bottom, jnp.zeros_like(xhalo), xhalo[...])
-    got = dot(p0[0:48, 0:32], rim).astype(BF)
-    for e in range(3):
-        for u in range(16):
-            xe[0, e, u + 1] = got[e * 16 : (e + 1) * 16, u * 128 : (u + 1) * 128]
-    conv_first(0)
+    finish_first(0, local_first + jnp.where(bottom, 0.0, xhalo[...].astype(F32)))
 
     def place_taps(got, plane):
         for o in range(2):
@@ -456,8 +497,7 @@
     halo_hid.wait_recv()
     rim = jnp.where(bottom, jnp.zeros_like(hhalo), hhalo[...])
     place_taps(dot(p1[...], rim).astype(BF), 0)
-    to_core_second.wait_recv()
-    for copy in others_second:
+    for copy in [to_core2] + passed[2:]:
         copy.wait_recv()
 
     linear = dot(l2[...], w2g[...])
@@ -524,26 +564,30 @@
     spread_delta(2)
     hidden_delta(1)
 
-    flat1 = jnp.concatenate([d1e[o, 0, 0:16].reshape(256, 128) for o in range(4)], axis=0)
-
-    @pl.loop(0, 9)
-    def _(t):
-        a, e = t // 3, t % 3
-        left = jnp.concatenate(
-            [
-                jnp.concatenate(
-                    [xe[2 * o + a, e, 0:16].reshape(256, 128), xe[2 * o + a, e, 1:17].reshape(256, 128)], axis=1
+    def first_gradient(start, stop, shift):
+        right = jnp.concatenate([d1e[o + shift, 0, 0:16].reshape(256, 128) for o in range(4)], axis=0)
+
+        @pl.loop(start, stop)
+        def _(t):
+            a, e = t // 3, t % 3
+            left = []
+            for o in range(4):
+                plane = 2 * (o + shift) + a
+                left.append(
+                    jnp.concatenate(
+                        [xe[plane, e, 0:16].reshape(256, 128), xe[plane, e, 1:17].reshape(256, 128)], axis=1
+                    )
                 )
-                for o in range(4)
-            ],
-            axis=0,
-        )
-        got = dot(left, flat1, 0, 0)
-        for k in range(24):
-            block = t * 24 + k
-            g = block % 54 // 7
-            s1[block // 54, g, block % 54 % 7] = got[64 + k * 8 : 64 + (k + 1) * 8].astype(BF)
-
+            got = dot(jnp.concatenate(left, axis=0), right, 0, 0)
+            for k in range(24):
+                block = t * 24 + k
+                g = block % 54 // 7
+                s1[block // 54, g, block % 54 % 7] = got[64 + k * 8 : 64 + (k + 1) * 8].astype(BF)
+
+    first_gradient(3, 9, 0)
+    halo_d1.wait_recv()
+    d1e[4, 0, 0:16] = jnp.where(top, jnp.zeros((16, 16, 128), BF), d1e[4, 0, 0:16])
+    first_gradient(0, 3, 1)
     sum1.cores()
 
     def shift_delta(first, count):
@@ -570,9 +614,8 @@
     shift_delta(2, 2)
     input_delta(0, 0)
     sum1.along_z()
+    sum2.turn()
     input_delta(0, 1)
-    halo_d1.wait_recv()
-    d1e[4, 0, 0:16] = jnp.where(top, jnp.zeros((16, 16, 128), BF), d1e[4, 0, 0:16])
     shift_delta(4, 1)
     input_delta(1, 0)
     input_delta(1, 1)
@@ -616,7 +659,8 @@
         out_specs=(vmem,) * 4,
         scratch_shapes=[
             pltpu.VMEM((9, 3, 17, 16, 128), BF),
-            pltpu.VMEM((32, 2048), BF),
+            pltpu.VMEM((256, 128), BF),
+            pltpu.VMEM((256, 128), BF),
             pltpu.VMEM((1728, 128), BF),
             pltpu.VMEM((2304, 128), BF),
             pltpu.VMEM((2304, 128), BF),
@@ -629,7 +673,7 @@
             pltpu.VMEM((3, 4, 64, 256), BF),
             pltpu.VMEM((5, 2, 17, 16, 128), BF),
             pltpu.VMEM((8, 32, 2048), BF),
-            pltpu.SemaphoreType.DMA((2, 10)),
+            pltpu.SemaphoreType.DMA((2, 14)),
             pltpu.SemaphoreType.DMA((2, 4)),
         ]
         + LineReduction.scratch(PIECE1)

time: 62.4 us -> 60.6 us (0.971)
  Pallas kernels: 60.8 us -> 59.1 us
    pallas_call x1, Pallas kernels: 58.8 us -> 57.1 us  [local(): pl.pallas_call(step_kernel, out_shape=(OUT((2, 8, 2048), BF), OUT((256, 2...]
where the time goes in v5:
time: 60.6 us; the launch traced here: 59.8 us
  Pallas kernels  59.1 us (98%)
  between operations  0.64 us (1%)
    pallas_call x1, Pallas kernels, local(): pl.pallas_call(step_kernel, out_shape=(OUT((2, 8, 2048), BF), OUT((256, 2...  57.1 us
    pallas_call x1, Pallas kernels, local(): pl.pallas_call(body, out_shape=(shape((2, 8, 2048), BF), shape((256, 2048...  1.98 us

profile of v5, /device:TPU:8, one launch (start us, length us, event | category | flops | bytes accessed | tf_op | source)
XLA Modules:
  0.0 59.8 jit_solution(1710595971835177501)
XLA Ops:
  0.6 57.1 %step.1 = (bf16[2,8,2048]{2,1,0:T(8,128)(2,1)S(1)}, bf16[256,2048]{1,0:T(8,128)(2,1)S(1)}, bf16[8,8,8,128]{3,2,1,0:T(8,128)(2,1)S(1)}, bf16[4,2,8,32,128]{4,3,2,1,0:T(8,128)(2,1)S(1)}) custom-call(bf16[256,2048]{1,0:T(8,128)(2,1)} %bitcast.4, bf16[432,128]{1,0:T(8,128)(2,1)} %w1.1, bf16[864,256]{1,0:T(8,128)(2,1)} %w2.1, bf16[2,8,2048]{2,1,0:T(8,128)(2,1)} %bitcast.5, ...), custom_call_target="tpu_custom_call" | custom-call | tf_op jit(solution)/shard_map/step/pallas_call | solution.py:650
  57.8 2.0 %finish.1 = (bf16[2,8,2048]{2,1,0:T(8,128)(2,1)}, bf16[256,2048]{1,0:T(8,128)(2,1)}, f32[432,128]{1,0:T(8,128)}, f32[864,256]{1,0:T(8,128)}) custom-call(bf16[2,8,2048]{2,1,0:T(8,128)(2,1)S(1)} %get-tuple-element.12.refs_0_, bf16[256,2048]{1,0:T(8,128)(2,1)S(1)} %get-tuple-element.13.refs_1_, bf16[8,8,8,128]{3,2,1,0:T(8,128)(2,1)S(1)} %get-tuple-element.14.refs_2_, ...), custom_call_target="tpu_custom_call" | custom-call | tf_op jit(solution)/shard_map/finish/pallas_call | solution.py:711

commit v6 on v5

--- a/solution.py
+++ b/solution.py
@@ -617,13 +617,7 @@
     sum2.turn()
     input_delta(0, 1)
     shift_delta(4, 1)
-    input_delta(1, 0)
-    input_delta(1, 1)
-
-    @pl.loop(0, 8)
-    def _(c):
-        lanes = pl.ds(pl.multiple_of(c * 256, 256), 256)
-        ig[:, lanes] = dot(p4[...], un[:, :, lanes].reshape(256, 256)).astype(BF)
+
 
     sum2.along_z()
     sum1.plane()
@@ -631,6 +625,14 @@
     sum1.gather_plane()
     sum2.gather_plane()
     sum1.gather_z()
+    input_delta(1, 0)
+    input_delta(1, 1)
+
+    @pl.loop(0, 8)
+    def _(c):
+        lanes = pl.ds(pl.multiple_of(c * 256, 256), 256)
+        ig[:, lanes] = dot(p4[...], un[:, :, lanes].reshape(256, 256)).astype(BF)
+
     sum2.finish()
     sum1.finish()
     for copy in sent + passed + [halo_in, halo_hid, halo_d2, halo_d1]:

time: 60.6 us -> 60 us (0.990)
  no operation moved by 1% of the time
where the time goes in v6:
time: 60 us; the launch traced here: 59.7 us
  Pallas kernels  59 us (98%)
  between operations  0.64 us (1%)
    pallas_call x1, Pallas kernels, local(): pl.pallas_call(step_kernel, out_shape=(OUT((2, 8, 2048), BF), OUT((256, 2...  57 us
    pallas_call x1, Pallas kernels, local(): pl.pallas_call(body, out_shape=(shape((2, 8, 2048), BF), shape((256, 2048...  1.98 us

profile of v6, /device:TPU:8, one launch (start us, length us, event | category | flops | bytes accessed | tf_op | source)
XLA Modules:
  0.0 59.7 jit_solution(5173786229307356446)
XLA Ops:
  0.6 57.0 %step.1 = (bf16[2,8,2048]{2,1,0:T(8,128)(2,1)S(1)}, bf16[256,2048]{1,0:T(8,128)(2,1)S(1)}, bf16[8,8,8,128]{3,2,1,0:T(8,128)(2,1)S(1)}, bf16[4,2,8,32,128]{4,3,2,1,0:T(8,128)(2,1)S(1)}) custom-call(bf16[256,2048]{1,0:T(8,128)(2,1)} %bitcast.4, bf16[432,128]{1,0:T(8,128)(2,1)} %w1.1, bf16[864,256]{1,0:T(8,128)(2,1)} %w2.1, bf16[2,8,2048]{2,1,0:T(8,128)(2,1)} %bitcast.5, ...), custom_call_target="tpu_custom_call" | custom-call | tf_op jit(solution)/shard_map/step/pallas_call | solution.py:652
  57.7 2.0 %finish.1 = (bf16[2,8,2048]{2,1,0:T(8,128)(2,1)}, bf16[256,2048]{1,0:T(8,128)(2,1)}, f32[432,128]{1,0:T(8,128)}, f32[864,256]{1,0:T(8,128)}) custom-call(bf16[2,8,2048]{2,1,0:T(8,128)(2,1)S(1)} %get-tuple-element.12.refs_0_, bf16[256,2048]{1,0:T(8,128)(2,1)S(1)} %get-tuple-element.13.refs_1_, bf16[8,8,8,128]{3,2,1,0:T(8,128)(2,1)S(1)} %get-tuple-element.14.refs_2_, ...), custom_call_target="tpu_custom_call" | custom-call | tf_op jit(solution)/shard_map/finish/pallas_call | solution.py:713
